TPU v7x, 256 devices: a whole 4x4x8 slice. The times are simulated.
256 devices in a mesh: seq: 32 (over y, z), ch: 8 (over x, core).
Axes of the slice: x: 4, y: 4, z: 8, core: 2. Of those that a mesh axis runs over, the one named last changes fastest.
Arguments:
- query_input: bfloat16 [4096, 4096], P('seq', 'ch'), may hold values from -6 to 6
- key_input: bfloat16 [4096, 4096], P('seq', 'ch'), may hold values from -6 to 6
- value_input: bfloat16 [4096, 4096], P('seq', 'ch'), may hold values from -6 to 6
- cotangent: bfloat16 [4096, 4096], P('seq', 'ch'), may hold values from -6 to 6
- filter_taps: float32 [4096, 4096], P('seq', 'ch'), may hold values from -0.09375 to 0.09375
- skip_gain: float32 [4096], P('ch'), may hold values from -2 to 2
Outputs:
- output: bfloat16 [4096, 4096], P('seq', 'ch')
- query_grad: bfloat16 [4096, 4096], P('seq', 'ch')
- key_grad: bfloat16 [4096, 4096], P('seq', 'ch')
- value_grad: bfloat16 [4096, 4096], P('seq', 'ch')
- filter_grad: float32 [4096, 4096], P('seq', 'ch')
- skip_grad: float32 [4096], P('ch')
- grad_rms: float32 [], replicated
All inputs are finite; a program needn't handle non-finite values.
Results may differ from a plain program's by a relative error of at most 0.0014.
Values sent between devices are 32-bit elements; how exact they have to be, the bound alone decides.
No kernel may reach another device: no remote copies, remote signals or barrier semaphores. Data moves between devices by JAX's collectives and lax.ppermute only.
A program may use at most 64 MiB of HBM per device.

v0:
```python
import math

import jax
import jax.numpy as jnp
import numpy as np
from jax import lax
from jax.experimental import pallas as pl
from jax.experimental.pallas import tpu as pltpu
from jax.sharding import PartitionSpec as P

ROWS = 128
BLOCKS = 32
LENGTH = ROWS * BLOCKS
CH_EACH = 16
LINES = 3 * CH_EACH
GROUP = 8


def tables():
    n2 = np.arange(ROWS)
    k1 = np.arange(BLOCKS)
    angle = 2.0 * np.pi * n2[None, :] * (k1[:, None] + 0.25) / LENGTH
    twiddle = np.stack([np.cos(angle), -np.sin(angle)]).astype(np.float32)
    angle = 2.0 * np.pi * ((n2[:, None] * n2[None, :]) % ROWS) / ROWS
    cosine, sine = np.cos(angle), np.sin(angle)
    whole = np.block([[cosine, -sine], [sine, cosine]]).astype(np.float32)
    high = whole.astype(jnp.bfloat16)
    low = (whole - high.astype(np.float32)).astype(jnp.bfloat16)
    return twiddle, np.stack([high, low])


def times(value, angle):
    re, im = value
    turn = round(angle / (math.pi / 4), 9) % 8
    half = math.sqrt(0.5)
    if turn == 0:
        return re, im
    if turn == 2:
        return im, -re
    if turn == 1:
        return (re + im) * half, (im - re) * half
    if turn == 3:
        return (im - re) * half, -(re + im) * half
    c, s = math.cos(angle), math.sin(angle)
    return re * c + im * s, im * c - re * s


def add(a, b):
    return a[0] + b[0], a[1] + b[1]


def sub(a, b):
    return a[0] - b[0], a[1] - b[1]


def split_radix(values):
    count = len(values)
    if count == 1:
        return values
    if count == 2:
        return [add(*values), sub(*values)]
    even = split_radix(values[0::2])
    first = split_radix(values[1::4])
    third = split_radix(values[3::4])
    quarter = count // 4
    out = [None] * count
    for k in range(quarter):
        one = times(first[k], 2 * math.pi * k / count)
        two = times(third[k], 2 * math.pi * 3 * k / count)
        total, diff = add(one, two), sub(one, two)
        out[k] = add(even[k], total)
        out[k + 2 * quarter] = sub(even[k], total)
        e_re, e_im = even[k + quarter]
        out[k + quarter] = (e_re + diff[1], e_im - diff[0])
        out[k + 3 * quarter] = (e_re - diff[1], e_im + diff[0])
    return out


def pre_kernel(q_ref, k_ref, v_ref, cot_ref, taps_ref, out_ref, skip_ref):
    mixed = k_ref[...].astype(jnp.float32) * v_ref[...].astype(jnp.float32)
    gated = q_ref[...].astype(jnp.float32) * cot_ref[...].astype(jnp.float32)
    skip_ref[...] = jnp.sum(mixed * gated, axis=0, keepdims=True)
    for index, signal in enumerate((mixed, gated, taps_ref[...])):
        lines = signal.T.reshape(BLOCKS, CH_EACH, ROWS)
        out_ref[:, index * CH_EACH : (index + 1) * CH_EACH, :] = lines


def split(value):
    high = value.astype(jnp.bfloat16)
    low = (value - high.astype(jnp.float32)).astype(jnp.bfloat16)
    return high, low


def dft_rows(value, mat_ref):
    high, low = split(value)

    def dot(left, right):
        return jnp.dot(left, right, preferred_element_type=jnp.float32)

    return dot(high, mat_ref[0]) + (dot(low, mat_ref[0]) + dot(high, mat_ref[1]))


def main_kernel(in_ref, tw_ref, mat_ref, out_ref, sq_ref, mid_ref):
    @pl.loop(0, LINES // 8)
    def _(step):
        lines = pl.ds(pl.multiple_of(step * 8, 8), 8)
        values = []
        for s in range(BLOCKS):
            signal = in_ref[s, lines, :]
            angle = 2 * math.pi * s / (4 * BLOCKS)
            values.append((signal * math.cos(angle), signal * -math.sin(angle)))
        for k1, (re, im) in enumerate(split_radix(values)):
            t_re, t_im = tw_ref[0, k1 : k1 + 1, :], tw_ref[1, k1 : k1 + 1, :]
            mid_ref[k1, lines, :ROWS] = re * t_re - im * t_im
            mid_ref[k1, lines, ROWS:] = re * t_im + im * t_re

    @pl.loop(0, BLOCKS // GROUP)
    def _(step):
        first = pl.multiple_of(step * GROUP, GROUP)
        here = pl.ds(first, GROUP)
        held = mid_ref[here].reshape(GROUP * LINES, 2 * ROWS)
        spectrum = dft_rows(held, mat_ref).reshape(GROUP, LINES, 2 * ROWS)
        re, im = spectrum[:, :, :ROWS], spectrum[:, :, ROWS:]
        x_re, g_re, h_re = (re[:, i * CH_EACH : (i + 1) * CH_EACH] for i in range(3))
        x_im, g_im, h_im = (im[:, i * CH_EACH : (i + 1) * CH_EACH] for i in range(3))
        product = jnp.concatenate(
            [
                jnp.concatenate([x_re * h_re - x_im * h_im, -(x_re * h_im + x_im * h_re)], axis=2),
                jnp.concatenate([g_re * h_re + g_im * h_im, g_re * h_im - g_im * h_re], axis=2),
                jnp.concatenate([g_re * x_re + g_im * x_im, g_re * x_im - g_im * x_re], axis=2),
            ],
            axis=1,
        )
        back = dft_rows(product.reshape(GROUP * LINES, 2 * ROWS), mat_ref)
        back = back.reshape(GROUP, LINES, 2 * ROWS)
        re, im = back[:, :, :ROWS], back[:, :, ROWS:]
        t_re, t_im = tw_ref[0, here, :][:, None, :], tw_ref[1, here, :][:, None, :]
        mid_ref[here, :, :ROWS] = re * t_re - im * t_im
        mid_ref[here, :, ROWS:] = re * t_im + im * t_re

    squares = jnp.zeros((8, ROWS), jnp.float32)
    for index in range(3):
        scale = 1.0 / LENGTH if index < 2 else 1.0 / LENGTH / math.sqrt(LENGTH)
        for half in range(CH_EACH // 8):
            line = index * CH_EACH + half * 8
            lines = slice(line, line + 8)
            values = [
                (mid_ref[k1, lines, :ROWS], mid_ref[k1, lines, ROWS:]) for k1 in range(BLOCKS)
            ]
            for s, (re, im) in enumerate(split_radix(values)):
                angle = 2 * math.pi * s / (4 * BLOCKS)
                series = re * (math.cos(angle) * scale) + im * (math.sin(angle) * scale)
                out_ref[s, lines, :] = series
                if index == 2:
                    squares = squares + series * series
    sq_ref[...] = squares


def post_kernel(
    in_ref, q_ref, k_ref, v_ref, cot_ref, gain_ref, out_ref, dq_ref, dk_ref, dv_ref, dh_ref
):
    def series(index):
        lines = in_ref[:, index * CH_EACH : (index + 1) * CH_EACH, :]
        return lines.reshape(BLOCKS * CH_EACH, ROWS).T

    query = q_ref[...].astype(jnp.float32)
    key = k_ref[...].astype(jnp.float32)
    value = v_ref[...].astype(jnp.float32)
    cot = cot_ref[...].astype(jnp.float32)
    gain = gain_ref[...]
    inner = series(0) + gain * (key * value)
    out_ref[...] = (query * inner).astype(jnp.bfloat16)
    dq_ref[...] = (cot * inner).astype(jnp.bfloat16)
    mixed_grad = series(1) + gain * (query * cot)
    dk_ref[...] = (mixed_grad * value).astype(jnp.bfloat16)
    dv_ref[...] = (mixed_grad * key).astype(jnp.bfloat16)
    dh_ref[...] = series(2)


def everyone(array, axis, bits):
    count = lax.axis_size(axis)
    for bit in bits:
        array = array + lax.ppermute(array, axis, [(i, i ^ bit) for i in range(count)])
    return array


def f32(*shape):
    return jax.ShapeDtypeStruct(shape, jnp.float32)


PARAMS = pltpu.CompilerParams(vmem_limit_bytes=40 * 2**20)


def body(query, key, value, cotangent, taps, gain):
    rows, channels = query.shape
    twiddle, matrix = tables()
    packed, skip_part = pl.pallas_call(
        pre_kernel,
        out_shape=(f32(BLOCKS, LINES, ROWS), f32(1, channels)),
        compiler_params=PARAMS,
    )(query, key, value, cotangent, taps)
    packed = lax.all_to_all(packed, "seq", 0, 0, tiled=True)
    time_scale = 1.0 / math.sqrt(LENGTH)
    skip_grad = everyone(skip_part, "seq", (1, 2, 4, 8, 16))[0] * time_scale
    results, squares = pl.pallas_call(
        main_kernel,
        out_shape=(f32(BLOCKS, LINES, ROWS), f32(8, ROWS)),
        scratch_shapes=[pltpu.VMEM((BLOCKS, LINES, 2 * ROWS), jnp.float32)],
        compiler_params=PARAMS,
    )(packed, twiddle, matrix)
    results = lax.all_to_all(results, "seq", 0, 0, tiled=True)
    total = jnp.sum(everyone(squares, "seq", (1, 2, 4, 8, 16))) + jnp.sum(skip_grad * skip_grad)
    total = everyone(total[None], "ch", (1, 2, 4))[0]
    grad_rms = jnp.sqrt(total / (channels * lax.axis_size("ch") * (LENGTH + 1)))
    bf16 = jax.ShapeDtypeStruct((rows, channels), jnp.bfloat16)
    output, query_grad, key_grad, value_grad, filter_grad = pl.pallas_call(
        post_kernel,
        out_shape=(bf16, bf16, bf16, bf16, f32(rows, channels)),
        compiler_params=PARAMS,
    )(results, query, key, value, cotangent, gain[None, :])
    return output, query_grad, key_grad, value_grad, filter_grad, skip_grad, grad_rms


def solution(mesh):
    both = P("seq", "ch")
    return jax.shard_map(
        body,
        mesh=mesh,
        in_specs=(both, both, both, both, both, P("ch")),
        out_specs=(both, both, both, both, both, P("ch"), P()),
        check_vma=False,
    )
```

profile of v0, /device:TPU:32, one launch (start us, length us, event | category | flops | bytes accessed | tf_op | source)
XLA Modules:
  0.0 113.8 jit_solution(1858911003999135979)
XLA Ops:
  1.5 0.9 copy-done.2
  2.4 0.9 copy-done.4
  4.3 0.9 copy-done.8
  5.5 34.5 %all_to_all.10.in_ref = f32[32,48,128]{2,1,0:T(8,128)S(1)} all-to-all(f32[32,48,128]{2,1,0:T(8,128)S(1)} %get-tuple-element.16), channel_id=1, replica_groups=mesh['seq'=32,'ch'=8] {'seq'}, dimensions={0} | all-to-all | bytes 1572864 | tf_op jit(solution)/shard_map/all_to_all | solution.py:202
  40.0 5.3 %shard_map.136 = (f32[32,48,128]{2,1,0:T(8,128)}, f32[8,128]{1,0:T(8,128)S(1)}) custom-call(f32[32,48,128]{2,1,0:T(8,128)S(1)} %all_to_all.10.in_ref, f32[2,32,128]{2,1,0:T(8,128)S(1)} %copy-done.10, bf16[2,256,256]{2,1,0:T(8,128)(2,1)S(1)} %copy-done.9), custom_call_target="tpu_custom_call" | custom-call | tf_op jit(solution)/shard_map/pallas_call | solution.py:205
  45.2 5.1 %all-to-all-start.1 = ((f32[32,48,128]{2,1,0:T(8,128)}), f32[32,48,128]{2,1,0:T(8,128)S(1)}, u32[]{:S(2)}, u32[]{:S(2)}) async-start(f32[32,48,128]{2,1,0:T(8,128)} %get-tuple-element.17), calls=%async_computation.1 | async-start | bytes 1572864 | tf_op jit(solution)/shard_map/all_to_all | solution.py:211
  50.6 1.8 %collective-permute-start = (f32[1,512]{1,0:T(1,128)S(1)}, f32[1,512]{1,0:T(1,128)S(1)}, u32[]{:S(2)}, u32[]{:S(2)}) collective-permute-start(f32[1,512]{1,0:T(1,128)S(1)} %get-tuple-element.23), channel_id=1, source_target_pairs={{0,8},{8,0},{16,24},{24,16},{32,40},{40,32},{48,56},{56,48},{64,72... | collective-permute-start | bytes 6152 | tf_op jit(solution)/shard_map/ppermute | solution.py:183
  52.4 13.8 %collective-permute-done.5 = f32[8,128]{1,0:T(8,128)S(1)} collective-permute-done((f32[8,128]{1,0:T(8,128)S(1)}, f32[8,128]{1,0:T(8,128)S(1)}, u32[]{:S(2)}, u32[]{:S(2)}) %collective-permute-start.5) | collective-permute-done | bytes 4128 | tf_op jit(solution)/shard_map/ppermute | solution.py:183
  66.3 3.5 %collective-permute-start.6 = (f32[8,128]{1,0:T(8,128)S(1)}, f32[8,128]{1,0:T(8,128)S(1)}, u32[]{:S(2)}, u32[]{:S(2)}) collective-permute-start(f32[8,128]{1,0:T(8,128)S(1)} %add.47), channel_id=1, source_target_pairs={{0,16},{8,24},{16,0},{24,8},{32,48},{40,56},{48,32},{56,40},{64,80... | collective-permute-start | bytes 12296 | tf_op jit(solution)/shard_map/ppermute | solution.py:183
  69.9 4.5 %collective-permute-done.1 = f32[1,512]{1,0:T(1,128)S(1)} collective-permute-done((f32[1,512]{1,0:T(1,128)S(1)}, f32[1,512]{1,0:T(1,128)S(1)}, u32[]{:S(2)}, u32[]{:S(2)}) %collective-permute-start.1) | collective-permute-done | bytes 2080 | tf_op jit(solution)/shard_map/ppermute | solution.py:183
  74.4 3.3 %collective-permute-start.2 = (f32[1,512]{1,0:T(1,128)S(1)}, f32[1,512]{1,0:T(1,128)S(1)}, u32[]{:S(2)}, u32[]{:S(2)}) collective-permute-start(f32[1,512]{1,0:T(1,128)S(1)} %add.43), channel_id=1, source_target_pairs={{0,32},{8,40},{16,48},{24,56},{32,0},{40,8},{48,16},{56,24},{64,96... | collective-permute-start | bytes 6152 | tf_op jit(solution)/shard_map/ppermute | solution.py:183
  77.6 2.7 %collective-permute-start.7 = (f32[8,128]{1,0:T(8,128)S(1)}, f32[8,128]{1,0:T(8,128)S(1)}, u32[]{:S(2)}, u32[]{:S(2)}) collective-permute-start(f32[8,128]{1,0:T(8,128)S(1)} %add.48), channel_id=1, source_target_pairs={{0,32},{8,40},{16,48},{24,56},{32,0},{40,8},{48,16},{56,24},{64,96... | collective-permute-start | bytes 12296 | tf_op jit(solution)/shard_map/ppermute | solution.py:183
  80.3 1.6 %collective-permute-done.2 = f32[1,512]{1,0:T(1,128)S(1)} collective-permute-done((f32[1,512]{1,0:T(1,128)S(1)}, f32[1,512]{1,0:T(1,128)S(1)}, u32[]{:S(2)}, u32[]{:S(2)}) %collective-permute-start.2) | collective-permute-done | bytes 2080 | tf_op jit(solution)/shard_map/ppermute | solution.py:183
  81.8 1.6 %collective-permute-start.3 = (f32[1,512]{1,0:T(1,128)S(1)}, f32[1,512]{1,0:T(1,128)S(1)}, u32[]{:S(2)}, u32[]{:S(2)}) collective-permute-start(f32[1,512]{1,0:T(1,128)S(1)} %add.44), channel_id=1, source_target_pairs={{0,64},{8,72},{16,80},{24,88},{32,96},{40,104},{48,112},{56,120},{... | collective-permute-start | bytes 6152 | tf_op jit(solution)/shard_map/ppermute | solution.py:183
  83.5 1.9 %collective-permute-done.3 = f32[1,512]{1,0:T(1,128)S(1)} collective-permute-done((f32[1,512]{1,0:T(1,128)S(1)}, f32[1,512]{1,0:T(1,128)S(1)}, u32[]{:S(2)}, u32[]{:S(2)}) %collective-permute-start.3) | collective-permute-done | bytes 2080 | tf_op jit(solution)/shard_map/ppermute | solution.py:183
  85.4 3.1 %collective-permute-start.4 = (f32[1,512]{1,0:T(1,128)S(1)}, f32[1,512]{1,0:T(1,128)S(1)}, u32[]{:S(2)}, u32[]{:S(2)}) collective-permute-start(f32[1,512]{1,0:T(1,128)S(1)} %add.45), channel_id=1, source_target_pairs={{0,128},{8,136},{16,144},{24,152},{32,160},{40,168},{48,176},{56,1... | collective-permute-start | bytes 6152 | tf_op jit(solution)/shard_map/ppermute | solution.py:183
  89.2 1.3 %collective-permute-done.4 = f32[1,512]{1,0:T(1,128)S(1)} collective-permute-done((f32[1,512]{1,0:T(1,128)S(1)}, f32[1,512]{1,0:T(1,128)S(1)}, u32[]{:S(2)}, u32[]{:S(2)}) %collective-permute-start.4) | collective-permute-done | bytes 2080 | tf_op jit(solution)/shard_map/ppermute | solution.py:183
  90.5 1.7 %collective-permute-done.8 = f32[8,128]{1,0:T(8,128)S(1)} collective-permute-done((f32[8,128]{1,0:T(8,128)S(1)}, f32[8,128]{1,0:T(8,128)S(1)}, u32[]{:S(2)}, u32[]{:S(2)}) %collective-permute-start.8) | collective-permute-done | bytes 4128 | tf_op jit(solution)/shard_map/ppermute | solution.py:183
  92.2 1.6 %collective-permute-start.9 = (f32[8,128]{1,0:T(8,128)S(1)}, f32[8,128]{1,0:T(8,128)S(1)}, u32[]{:S(2)}, u32[]{:S(2)}) collective-permute-start(f32[8,128]{1,0:T(8,128)S(1)} %add.50), channel_id=1, source_target_pairs={{0,128},{8,136},{16,144},{24,152},{32,160},{40,168},{48,176},{56,1... | collective-permute-start | bytes 12296 | tf_op jit(solution)/shard_map/ppermute | solution.py:183
  94.4 2.9 %collective-permute-done.9 = f32[8,128]{1,0:T(8,128)S(1)} collective-permute-done((f32[8,128]{1,0:T(8,128)S(1)}, f32[8,128]{1,0:T(8,128)S(1)}, u32[]{:S(2)}, u32[]{:S(2)}) %collective-permute-start.9) | collective-permute-done | bytes 4128 | tf_op jit(solution)/shard_map/ppermute | solution.py:183
  99.2 0.9 collective-permute-start.10
  101.0 2.9 %collective-permute-start.11 = (f32[1]{0:T(128)}, f32[1]{0:T(128)}, u32[]{:S(2)}, u32[]{:S(2)}) collective-permute-start(f32[1]{0:T(128)} %add.53), channel_id=1, source_target_pairs={{0,2},{1,3},{2,0},{3,1},{4,6},{5,7},{6,4},{7,5},{8,10},{9,11},{10,... | collective-permute-start | bytes 20 | tf_op jit(solution)/shard_map/ppermute | solution.py:183
  105.2 4.4 %collective-permute-start.12 = (f32[1]{0:T(128)}, f32[1]{0:T(128)}, u32[]{:S(2)}, u32[]{:S(2)}) collective-permute-start(f32[1]{0:T(128)} %add.54), channel_id=1, source_target_pairs={{0,4},{1,5},{2,6},{3,7},{4,0},{5,1},{6,2},{7,3},{8,12},{9,13},{10,... | collective-permute-start | bytes 20 | tf_op jit(solution)/shard_map/ppermute | solution.py:183
  111.6 1.1 shard_map.137
  (45 shorter events, 6.6 us)
Async XLA Ops:
  0.6 0.9 copy-start
  1.5 0.9 copy-start.2
  4.3 0.9 copy-start.8
  5.5 34.5 %copy-start.9 = (bf16[2,256,256]{2,1,0:T(8,128)(2,1)S(1)}, bf16[2,256,256]{2,1,0:T(8,128)(2,1)}, u32[]{:S(2)}) copy-start(bf16[2,256,256]{2,1,0:T(8,128)(2,1)} %constant.13.clone.mat_ref) | copy-start | bytes 786436
  5.5 34.5 %copy-start.10 = (f32[2,32,128]{2,1,0:T(8,128)S(1)}, f32[2,32,128]{2,1,0:T(8,128)}, u32[]{:S(2)}) copy-start(f32[2,32,128]{2,1,0:T(8,128)} %constant.12.clone.tw_ref) | copy-start | bytes 98308
  45.2 65.7 %copy-start.1 = (bf16[128,512]{1,0:T(8,128)(2,1)S(1)}, bf16[128,512]{1,0:T(8,128)(2,1)}, u32[]{:S(2)}) copy-start(bf16[128,512]{1,0:T(8,128)(2,1)} %q_ref.3) | copy-start | bytes 393220
  45.2 65.7 %copy-start.3 = (bf16[128,512]{1,0:T(8,128)(2,1)S(1)}, bf16[128,512]{1,0:T(8,128)(2,1)}, u32[]{:S(2)}) copy-start(bf16[128,512]{1,0:T(8,128)(2,1)} %k_ref.3) | copy-start | bytes 393220
  45.2 65.8 %copy-start.5 = (bf16[128,512]{1,0:T(8,128)(2,1)S(1)}, bf16[128,512]{1,0:T(8,128)(2,1)}, u32[]{:S(2)}) copy-start(bf16[128,512]{1,0:T(8,128)(2,1)} %v_ref.3) | copy-start | bytes 393220
  45.2 65.8 %copy-start.7 = (bf16[128,512]{1,0:T(8,128)(2,1)S(1)}, bf16[128,512]{1,0:T(8,128)(2,1)}, u32[]{:S(2)}) copy-start(bf16[128,512]{1,0:T(8,128)(2,1)} %cot_ref.3) | copy-start | bytes 393220
  45.2 65.7 %all-to-all-start.1 = ((f32[32,48,128]{2,1,0:T(8,128)}), f32[32,48,128]{2,1,0:T(8,128)S(1)}, u32[]{:S(2)}, u32[]{:S(2)}) async-start(f32[32,48,128]{2,1,0:T(8,128)} %get-tuple-element.17), calls=%async_computation.1 | async-start | bytes 1572864 | tf_op jit(solution)/shard_map/all_to_all | solution.py:211
  50.3 16.0 %collective-permute-start.5 = (f32[8,128]{1,0:T(8,128)S(1)}, f32[8,128]{1,0:T(8,128)S(1)}, u32[]{:S(2)}, u32[]{:S(2)}) collective-permute-start(f32[8,128]{1,0:T(8,128)S(1)} %get-tuple-element.24), channel_id=1, source_target_pairs={{0,8},{8,0},{16,24},{24,16},{32,40},{40,32},{48,56},{56,48},{64,72... | collective-permute-start | bytes 12296 | tf_op jit(solution)/shard_map/ppermute | solution.py:183
  50.6 19.1 %collective-permute-start = (f32[1,512]{1,0:T(1,128)S(1)}, f32[1,512]{1,0:T(1,128)S(1)}, u32[]{:S(2)}, u32[]{:S(2)}) collective-permute-start(f32[1,512]{1,0:T(1,128)S(1)} %get-tuple-element.23), channel_id=1, source_target_pairs={{0,8},{8,0},{16,24},{24,16},{32,40},{40,32},{48,56},{56,48},{64,72... | collective-permute-start | bytes 6152 | tf_op jit(solution)/shard_map/ppermute | solution.py:183
  66.3 11.4 %collective-permute-start.6 = (f32[8,128]{1,0:T(8,128)S(1)}, f32[8,128]{1,0:T(8,128)S(1)}, u32[]{:S(2)}, u32[]{:S(2)}) collective-permute-start(f32[8,128]{1,0:T(8,128)S(1)} %add.47), channel_id=1, source_target_pairs={{0,16},{8,24},{16,0},{24,8},{32,48},{40,56},{48,32},{56,40},{64,80... | collective-permute-start | bytes 12296 | tf_op jit(solution)/shard_map/ppermute | solution.py:183
  69.8 4.6 %collective-permute-start.1 = (f32[1,512]{1,0:T(1,128)S(1)}, f32[1,512]{1,0:T(1,128)S(1)}, u32[]{:S(2)}, u32[]{:S(2)}) collective-permute-start(f32[1,512]{1,0:T(1,128)S(1)} %add.42), channel_id=1, source_target_pairs={{0,16},{8,24},{16,0},{24,8},{32,48},{40,56},{48,32},{56,40},{64,80... | collective-permute-start | bytes 6152 | tf_op jit(solution)/shard_map/ppermute | solution.py:183
  74.4 7.5 %collective-permute-start.2 = (f32[1,512]{1,0:T(1,128)S(1)}, f32[1,512]{1,0:T(1,128)S(1)}, u32[]{:S(2)}, u32[]{:S(2)}) collective-permute-start(f32[1,512]{1,0:T(1,128)S(1)} %add.43), channel_id=1, source_target_pairs={{0,32},{8,40},{16,48},{24,56},{32,0},{40,8},{48,16},{56,24},{64,96... | collective-permute-start | bytes 6152 | tf_op jit(solution)/shard_map/ppermute | solution.py:183
  77.6 11.0 %collective-permute-start.7 = (f32[8,128]{1,0:T(8,128)S(1)}, f32[8,128]{1,0:T(8,128)S(1)}, u32[]{:S(2)}, u32[]{:S(2)}) collective-permute-start(f32[8,128]{1,0:T(8,128)S(1)} %add.48), channel_id=1, source_target_pairs={{0,32},{8,40},{16,48},{24,56},{32,0},{40,8},{48,16},{56,24},{64,96... | collective-permute-start | bytes 12296 | tf_op jit(solution)/shard_map/ppermute | solution.py:183
  81.8 3.6 %collective-permute-start.3 = (f32[1,512]{1,0:T(1,128)S(1)}, f32[1,512]{1,0:T(1,128)S(1)}, u32[]{:S(2)}, u32[]{:S(2)}) collective-permute-start(f32[1,512]{1,0:T(1,128)S(1)} %add.44), channel_id=1, source_target_pairs={{0,64},{8,72},{16,80},{24,88},{32,96},{40,104},{48,112},{56,120},{... | collective-permute-start | bytes 6152 | tf_op jit(solution)/shard_map/ppermute | solution.py:183
  85.4 5.1 %collective-permute-start.4 = (f32[1,512]{1,0:T(1,128)S(1)}, f32[1,512]{1,0:T(1,128)S(1)}, u32[]{:S(2)}, u32[]{:S(2)}) collective-permute-start(f32[1,512]{1,0:T(1,128)S(1)} %add.45), channel_id=1, source_target_pairs={{0,128},{8,136},{16,144},{24,152},{32,160},{40,168},{48,176},{56,1... | collective-permute-start | bytes 6152 | tf_op jit(solution)/shard_map/ppermute | solution.py:183
  88.6 3.6 %collective-permute-start.8 = (f32[8,128]{1,0:T(8,128)S(1)}, f32[8,128]{1,0:T(8,128)S(1)}, u32[]{:S(2)}, u32[]{:S(2)}) collective-permute-start(f32[8,128]{1,0:T(8,128)S(1)} %add.49), channel_id=1, source_target_pairs={{0,64},{8,72},{16,80},{24,88},{32,96},{40,104},{48,112},{56,120},{... | collective-permute-start | bytes 12296 | tf_op jit(solution)/shard_map/ppermute | solution.py:183
  90.5 3.3 %copy-start.12 = (f32[1,512]{1,0:T(1,128)}, f32[1,512]{1,0:T(1,128)S(1)}, u32[]{:S(2)}) copy-start(f32[1,512]{1,0:T(1,128)S(1)} %add_multiply_fusion) | copy-start | bytes 6148
  92.2 5.1 %collective-permute-start.9 = (f32[8,128]{1,0:T(8,128)S(1)}, f32[8,128]{1,0:T(8,128)S(1)}, u32[]{:S(2)}, u32[]{:S(2)}) collective-permute-start(f32[8,128]{1,0:T(8,128)S(1)} %add.50), channel_id=1, source_target_pairs={{0,128},{8,136},{16,144},{24,152},{32,160},{40,168},{48,176},{56,1... | collective-permute-start | bytes 12296 | tf_op jit(solution)/shard_map/ppermute | solution.py:183
  99.2 1.2 %collective-permute-start.10 = (f32[1]{0:T(128)}, f32[1]{0:T(128)}, u32[]{:S(2)}, u32[]{:S(2)}) collective-permute-start(f32[1]{0:T(128)} %bitcast.2), channel_id=1, source_target_pairs={{0,1},{1,0},{2,3},{3,2},{4,5},{5,4},{6,7},{7,6},{8,9},{9,8},{10,11... | collective-permute-start | bytes 20 | tf_op jit(solution)/shard_map/ppermute | solution.py:183
  101.0 3.6 %collective-permute-start.11 = (f32[1]{0:T(128)}, f32[1]{0:T(128)}, u32[]{:S(2)}, u32[]{:S(2)}) collective-permute-start(f32[1]{0:T(128)} %add.53), channel_id=1, source_target_pairs={{0,2},{1,3},{2,0},{3,1},{4,6},{5,7},{6,4},{7,5},{8,10},{9,11},{10,... | collective-permute-start | bytes 20 | tf_op jit(solution)/shard_map/ppermute | solution.py:183
  105.2 5.1 %collective-permute-start.12 = (f32[1]{0:T(128)}, f32[1]{0:T(128)}, u32[]{:S(2)}, u32[]{:S(2)}) collective-permute-start(f32[1]{0:T(128)} %add.54), channel_id=1, source_target_pairs={{0,4},{1,5},{2,6},{3,7},{4,0},{5,1},{6,2},{7,3},{8,12},{9,13},{10,... | collective-permute-start | bytes 20 | tf_op jit(solution)/shard_map/ppermute | solution.py:183
  (3 other events, 2.5 us)
where the time goes:
time: 114 us
  blocking collectives  34.5 us (30%)
  starting transfers between devices  31.9 us (28%)
  waiting for transfers between devices  29.4 us (26%)
  Pallas kernels  6.61 us (6%)
  local copies, waits for them, and re-layouts  5.18 us (5%)
  between operations  5.05 us (4%)
  other arithmetic  1.23 us (1%)
    all_to_all x1, blocking collectives, body(): packed = lax.all_to_all(packed, 'seq', 0, 0, tiled=True)  34.5 us
    ppermute x13, waiting for transfers between devices, everyone(): lax.ppermute(array, axis, [(i, i ^ bit) for i in range(count)])  29.4 us
    ppermute x13, starting transfers between devices, everyone(): lax.ppermute(array, axis, [(i, i ^ bit) for i in range(count)])  26.8 us
    pallas_call x1, Pallas kernels, body(): pl.pallas_call(main_kernel, out_shape=(f32(BLOCKS, LINES, ROWS), f32(8, R...  5.26 us
    unnamed x26, local copies, waits for them, and re-layouts  5.18 us
    all_to_all x1, starting transfers between devices, body(): results = lax.all_to_all(results, 'seq', 0, 0, tiled=True)  5.07 us
  transfers between devices with their start and end apart: 14, of which 10 were waited for; matrix products, arithmetic and copies ran while one was open for 1% of the time, Pallas kernels for 0%

commit v1 on v0

--- a/solution.py
+++ b/solution.py
@@ -14,6 +14,9 @@
 CH_EACH = 16
 LINES = 3 * CH_EACH
 GROUP = 8
+BACK = LINES + 1
+ORDER = list(range(BLOCKS))
+PLACE = [ORDER.index(s) for s in range(BLOCKS)]
 
 
 def tables():
@@ -76,13 +79,30 @@
     return out
 
 
-def pre_kernel(q_ref, k_ref, v_ref, cot_ref, taps_ref, out_ref, skip_ref):
-    mixed = k_ref[...].astype(jnp.float32) * v_ref[...].astype(jnp.float32)
-    gated = q_ref[...].astype(jnp.float32) * cot_ref[...].astype(jnp.float32)
-    skip_ref[...] = jnp.sum(mixed * gated, axis=0, keepdims=True)
-    for index, signal in enumerate((mixed, gated, taps_ref[...])):
+def pre_kernel(q_hbm, k_hbm, v_hbm, cot_hbm, taps_hbm, out_hbm, *scratch):
+    buffers, out_ref, in_sems, out_sems = scratch[:5], *scratch[5:]
+    sources = (q_hbm, k_hbm, v_hbm, cot_hbm, taps_hbm)
+    loads = [pltpu.make_async_copy(sources[i], buffers[i], in_sems.at[i]) for i in range(5)]
+    for i in (4, 1, 2, 0, 3):
+        loads[i].start()
+    stores = []
+    for index, needs in ((2, (4,)), (0, (1, 2)), (1, (0, 3))):
+        signal = None
+        for i in needs:
+            loads[i].wait()
+            factor = buffers[i][...].astype(jnp.float32)
+            signal = factor if signal is None else signal * factor
         lines = signal.T.reshape(BLOCKS, CH_EACH, ROWS)
-        out_ref[:, index * CH_EACH : (index + 1) * CH_EACH, :] = lines
+        for s in range(BLOCKS):
+            out_ref[index, PLACE[s]] = lines[s]
+        here = slice(index * CH_EACH, (index + 1) * CH_EACH)
+        store = pltpu.make_async_copy(
+            out_ref.at[index], out_hbm.at[:, here, :], out_sems.at[index]
+        )
+        store.start()
+        stores.append(store)
+    for store in stores:
+        store.wait()
 
 
 def split(value):
@@ -100,13 +120,13 @@
     return dot(high, mat_ref[0]) + (dot(low, mat_ref[0]) + dot(high, mat_ref[1]))
 
 
-def main_kernel(in_ref, tw_ref, mat_ref, out_ref, sq_ref, mid_ref):
+def main_kernel(in_ref, tw_ref, mat_ref, out_ref, mid_ref):
     @pl.loop(0, LINES // 8)
     def _(step):
         lines = pl.ds(pl.multiple_of(step * 8, 8), 8)
         values = []
         for s in range(BLOCKS):
-            signal = in_ref[s, lines, :]
+            signal = in_ref[PLACE[s], lines, :]
             angle = 2 * math.pi * s / (4 * BLOCKS)
             values.append((signal * math.cos(angle), signal * -math.sin(angle)))
         for k1, (re, im) in enumerate(split_radix(values)):
@@ -150,18 +170,45 @@
             for s, (re, im) in enumerate(split_radix(values)):
                 angle = 2 * math.pi * s / (4 * BLOCKS)
                 series = re * (math.cos(angle) * scale) + im * (math.sin(angle) * scale)
-                out_ref[s, lines, :] = series
+                out_ref[PLACE[s] * BACK + line : PLACE[s] * BACK + line + 8, :] = series
                 if index == 2:
                     squares = squares + series * series
-    sq_ref[...] = squares
+
+    direct = jnp.zeros((CH_EACH, ROWS), jnp.float32)
+    for s in range(BLOCKS):
+        direct = direct + in_ref[s, :CH_EACH, :] * in_ref[s, CH_EACH : 2 * CH_EACH, :]
+    direct = jnp.sum(direct, axis=1, keepdims=True) * (1.0 / math.sqrt(LENGTH))
+    row = lax.broadcasted_iota(jnp.int32, (CH_EACH, ROWS), 0)
+    lane = lax.broadcasted_iota(jnp.int32, (CH_EACH, ROWS), 1)
+    last = jnp.sum(jnp.where(row == lane, direct, 0.0), axis=0, keepdims=True)
+    squares = jnp.sum(jnp.sum(squares, axis=0, keepdims=True), axis=1, keepdims=True)
+    last = jnp.where(lane[:1] == CH_EACH, squares, last)
+    for s in range(BLOCKS):
+        out_ref[s * BACK + LINES : (s + 1) * BACK, :] = last
+
+
+def stats_kernel(in_ref, skip_ref, sum_ref):
+    per_row = ROWS // CH_EACH
+    rows = BLOCKS // per_row
+    lane = lax.broadcasted_iota(jnp.int32, (rows, ROWS), 1)
+    skip = jnp.zeros((rows, ROWS), jnp.float32)
+    squares = jnp.zeros((rows, ROWS), jnp.float32)
+    for m in range(per_row):
+        at = [PLACE[r * per_row + m] * BACK + LINES for r in range(rows)]
+        lines = jnp.concatenate([in_ref[i : i + 1, :] for i in at], axis=0)
+        squares = squares + jnp.where(lane == CH_EACH, lines, 0.0)
+        moved = pltpu.roll(lines, m * CH_EACH, 1) if m else lines
+        skip = jnp.where(lane // CH_EACH == m, moved, skip)
+    skip_ref[...] = skip
+    sum_ref[...] = jnp.sum(squares + skip * skip, axis=0, keepdims=True)
 
 
 def post_kernel(
     in_ref, q_ref, k_ref, v_ref, cot_ref, gain_ref, out_ref, dq_ref, dk_ref, dv_ref, dh_ref
 ):
     def series(index):
-        lines = in_ref[:, index * CH_EACH : (index + 1) * CH_EACH, :]
-        return lines.reshape(BLOCKS * CH_EACH, ROWS).T
+        first = [PLACE[s] * BACK + index * CH_EACH for s in range(BLOCKS)]
+        return jnp.concatenate([in_ref[i : i + CH_EACH, :] for i in first], axis=0).T
 
     query = q_ref[...].astype(jnp.float32)
     key = k_ref[...].astype(jnp.float32)
@@ -177,11 +224,18 @@
     dh_ref[...] = series(2)
 
 
-def everyone(array, axis, bits):
-    count = lax.axis_size(axis)
-    for bit in bits:
-        array = array + lax.ppermute(array, axis, [(i, i ^ bit) for i in range(count)])
-    return array
+def partner(array, bit):
+    return lax.ppermute(array, "ch", [(i, i ^ bit) for i in range(lax.axis_size("ch"))])
+
+
+def over_channels(array):
+    array = array + partner(array, 1)
+    two, four, six = (partner(array, bit) for bit in (2, 4, 6))
+    return (array + two) + (four + six)
+
+
+def exchange(array):
+    return lax.all_to_all(array, "seq", 0, 0, axis_index_groups=[ORDER], tiled=True)
 
 
 def f32(*shape):
@@ -189,36 +243,57 @@
 
 
 PARAMS = pltpu.CompilerParams(vmem_limit_bytes=40 * 2**20)
+WIDE = pltpu.CompilerParams(vmem_limit_bytes=60 * 2**20)
 
 
 def body(query, key, value, cotangent, taps, gain):
     rows, channels = query.shape
     twiddle, matrix = tables()
-    packed, skip_part = pl.pallas_call(
+    signals = (query, key, value, cotangent, taps)
+    hbm = pl.BlockSpec(memory_space=pltpu.HBM)
+    packed = pl.pallas_call(
         pre_kernel,
-        out_shape=(f32(BLOCKS, LINES, ROWS), f32(1, channels)),
-        compiler_params=PARAMS,
-    )(query, key, value, cotangent, taps)
-    packed = lax.all_to_all(packed, "seq", 0, 0, tiled=True)
-    time_scale = 1.0 / math.sqrt(LENGTH)
-    skip_grad = everyone(skip_part, "seq", (1, 2, 4, 8, 16))[0] * time_scale
-    results, squares = pl.pallas_call(
+        out_shape=f32(BLOCKS, LINES, ROWS),
+        in_specs=[hbm] * len(signals),
+        out_specs=hbm,
+        scratch_shapes=[pltpu.VMEM(signal.shape, signal.dtype) for signal in signals]
+        + [
+            pltpu.VMEM((3, BLOCKS, CH_EACH, ROWS), jnp.float32),
+            pltpu.SemaphoreType.DMA((len(signals),)),
+            pltpu.SemaphoreType.DMA((3,)),
+        ],
+        compiler_params=WIDE,
+    )(*signals)
+    results = pl.pallas_call(
         main_kernel,
-        out_shape=(f32(BLOCKS, LINES, ROWS), f32(8, ROWS)),
+        out_shape=f32(BLOCKS * BACK, ROWS),
         scratch_shapes=[pltpu.VMEM((BLOCKS, LINES, 2 * ROWS), jnp.float32)],
         compiler_params=PARAMS,
-    )(packed, twiddle, matrix)
-    results = lax.all_to_all(results, "seq", 0, 0, tiled=True)
-    total = jnp.sum(everyone(squares, "seq", (1, 2, 4, 8, 16))) + jnp.sum(skip_grad * skip_grad)
-    total = everyone(total[None], "ch", (1, 2, 4))[0]
+    )(exchange(packed), twiddle, matrix)
+    results = exchange(results.reshape(BLOCKS, BACK, 1, ROWS)).reshape(BLOCKS * BACK, ROWS)
+    skip_grad, total = pl.pallas_call(
+        stats_kernel,
+        out_shape=(f32(channels // ROWS, ROWS), f32(1, ROWS)),
+        compiler_params=PARAMS,
+    )(results)
+    total = jnp.sum(over_channels(total))
     grad_rms = jnp.sqrt(total / (channels * lax.axis_size("ch") * (LENGTH + 1)))
     bf16 = jax.ShapeDtypeStruct((rows, channels), jnp.bfloat16)
     output, query_grad, key_grad, value_grad, filter_grad = pl.pallas_call(
         post_kernel,
         out_shape=(bf16, bf16, bf16, bf16, f32(rows, channels)),
         compiler_params=PARAMS,
+        cost_estimate=pl.CostEstimate(flops=10**6, bytes_accessed=2 * 10**6, transcendentals=0),
     )(results, query, key, value, cotangent, gain[None, :])
-    return output, query_grad, key_grad, value_grad, filter_grad, skip_grad, grad_rms
+    return (
+        output,
+        query_grad,
+        key_grad,
+        value_grad,
+        filter_grad,
+        skip_grad.reshape(channels),
+        grad_rms,
+    )
 
 
 def solution(mesh):

time: 114 us -> 82 us (0.72)
  blocking collectives: 34.5 us -> 62.4 us
  starting transfers between devices: 31.9 us -> 4.1 us
  waiting for transfers between devices: 29.4 us -> 3.71 us
  local copies, waits for them, and re-layouts: 5.18 us -> 0.03 us
  between operations: 5.05 us -> 2.51 us
  Pallas kernels: 6.61 us -> 8.31 us
    all_to_all x1 -> x2, blocking collectives: 34.5 us -> 62.4 us  [exchange(): lax.all_to_all(array, 'seq', 0, 0, axis_index_groups=[ORDER], tiled=True)]
    ppermute x13 -> x4, waiting for transfers between devices: 29.4 us -> 3.71 us  [partner(): lax.ppermute(array, 'ch', [(i, i ^ bit) for i in range(lax.axis_size('ch'...]
    ppermute x13 -> x4, starting transfers between devices: 26.8 us -> 4.1 us  [partner(): lax.ppermute(array, 'ch', [(i, i ^ bit) for i in range(lax.axis_size('ch'...]
    unnamed x26 -> x14, local copies, waits for them, and re-layouts: 5.18 us -> 0.03 us
    all_to_all x1 -> x0, starting transfers between devices: 5.07 us -> none  [body(): results = lax.all_to_all(results, 'seq', 0, 0, tiled=True)]
    pallas_call x2 -> x3, Pallas kernels: 5.52 us -> 7.21 us  [the longest x1 4.36 us: body(): pl.pallas_call(main_kernel, out_shape=f32(BLOCKS * BACK, ROWS), scratch_s...]
  transfers between devices with their start and end apart: 14 -> 4, of which waited for: 10 -> 2; matrix products, arithmetic and copies ran while one was open for 1% -> 0% of each run, Pallas kernels for 0% -> 1%
where the time goes in v1:
time: 82 us; the launch traced here: 81.7 us
  blocking collectives  62.4 us (76%)
  Pallas kernels  8.31 us (10%)
  starting transfers between devices  4.1 us (5%)
  waiting for transfers between devices  3.71 us (5%)
  between operations  2.51 us (3%)
    all_to_all x2, blocking collectives, exchange(): lax.all_to_all(array, 'seq', 0, 0, axis_index_groups=[ORDER], tiled=True)  62.4 us
    pallas_call x1, Pallas kernels, body(): pl.pallas_call(main_kernel, out_shape=f32(BLOCKS * BACK, ROWS), scratch_s...  4.36 us
    ppermute x4, starting transfers between devices, partner(): lax.ppermute(array, 'ch', [(i, i ^ bit) for i in range(lax.axis_size('ch'...  4.1 us
    ppermute x4, waiting for transfers between devices, partner(): lax.ppermute(array, 'ch', [(i, i ^ bit) for i in range(lax.axis_size('ch'...  3.71 us
    pallas_call x1, Pallas kernels, body(): pl.pallas_call(pre_kernel, out_shape=f32(BLOCKS, LINES, ROWS), in_specs=[...  2.19 us
  transfers between devices with their start and end apart: 4, of which 2 were waited for; matrix products, arithmetic and copies ran while one was open for 0% of the time, Pallas kernels for 1%

profile of v1, /device:TPU:32, one launch (start us, length us, event | category | flops | bytes accessed | tf_op | source)
XLA Modules:
  0.0 81.7 jit_solution(10012650946094969221)
XLA Ops:
  0.6 2.2 %shard_map.135 = f32[32,48,128]{2,1,0:T(8,128)} custom-call(bf16[128,512]{1,0:T(8,128)(2,1)} %q_ref.1, bf16[128,512]{1,0:T(8,128)(2,1)} %k_ref.1, bf16[128,512]{1,0:T(8,128)(2,1)} %v_ref.1, bf16[128,512]{1,0:T(8,128)(2,1)} %cot_ref.1, f32[128,512]{1,0:T(8,128)} %taps_hbm.1), custom_call_target="tpu_custom_call" | custom-call | tf_op jit(solution)/shard_map/pallas_call | solution.py:254
  2.8 0.0 copy-start.4
  2.8 0.0 copy-start.5
  2.9 34.7 %all_to_all.10.in_ref = f32[32,48,128]{2,1,0:T(8,128)S(1)} all-to-all(f32[32,48,128]{2,1,0:T(8,128)} %shard_map.135), channel_id=1, replica_groups={{0,8,16,24,32,40,48,56,64,72,80,88,96,104,112,120,128,136,144,152,160,1..., dimensions={0} | all-to-all | bytes 1572864 | tf_op jit(solution)/shard_map/all_to_all | solution.py:238
  37.5 0.0 copy-done.4
  37.5 0.0 copy-done.5
  37.5 4.4 %shard_map.136 = f32[1568,128]{1,0:T(8,128)S(1)} custom-call(f32[32,48,128]{2,1,0:T(8,128)S(1)} %all_to_all.10.in_ref, f32[2,32,128]{2,1,0:T(8,128)S(1)} %copy-done.5, bf16[2,256,256]{2,1,0:T(8,128)(2,1)S(1)} %copy-done.4), custom_call_target="tpu_custom_call" | custom-call | tf_op jit(solution)/shard_map/pallas_call | solution.py:267
  41.9 27.8 %all_to_all.11 = f32[32,49,1,128]{3,2,1,0:T(1,128)S(1)} all-to-all(f32[32,49,1,128]{3,2,1,0:T(1,128)S(1)} %bitcast.6), channel_id=1, replica_groups={{0,8,16,24,32,40,48,56,64,72,80,88,96,104,112,120,128,136,144,152,160,1..., dimensions={0} | all-to-all | bytes 1605632 | tf_op jit(solution)/shard_map/all_to_all | solution.py:238
  69.7 0.7 shard_map.138
  70.3 0.0 collective-permute-start
  70.3 1.1 %collective-permute-done = f32[1,128]{1,0:T(1,128)S(1)} collective-permute-done((f32[1,128]{1,0:T(1,128)S(1)}, f32[1,128]{1,0:T(1,128)S(1)}, u32[]{:S(2)}, u32[]{:S(2)}) %collective-permute-start) | collective-permute-done | bytes 544 | tf_op jit(solution)/shard_map/ppermute | solution.py:228
  71.4 2.8 %collective-permute-start.3 = (f32[1,128]{1,0:T(1,128)S(1)}, f32[1,128]{1,0:T(1,128)S(1)}, u32[]{:S(2)}, u32[]{:S(2)}) collective-permute-start(f32[1,128]{1,0:T(1,128)S(1)} %add.12), channel_id=1, source_target_pairs={{0,6},{1,7},{2,4},{3,5},{4,2},{5,3},{6,0},{7,1},{8,14},{9,15},{10,... | collective-permute-start | bytes 1544 | tf_op jit(solution)/shard_map/ppermute | solution.py:228
  74.2 0.8 collective-permute-start.2
  75.0 0.5 collective-permute-start.1
  75.5 0.0 copy-done
  75.5 0.0 copy-done.1
  75.5 0.0 copy-done.2
  75.6 0.0 copy-done.3
  75.6 0.0 copy-done.6
  75.6 1.1 %shard_map.137 = (bf16[128,512]{1,0:T(8,128)(2,1)}, bf16[128,512]{1,0:T(8,128)(2,1)}, bf16[128,512]{1,0:T(8,128)(2,1)}, bf16[128,512]{1,0:T(8,128)(2,1)}, f32[128,512]{1,0:T(8,128)}) custom-call(f32[1568,128]{1,0:T(8,128)S(1)} %bitcast.5, bf16[128,512]{1,0:T(8,128)(2,1)S(1)} %copy-done, bf16[128,512]{1,0:T(8,128)(2,1)S(1)} %copy-done.1, ...), custom_call_target="tpu_custom_call" | custom-call | flops 1000000 | bytes 2000000 | tf_op jit(solution)/shard_map/pallas_call | solution.py:282
  76.7 0.0 collective-permute-done.3
  76.7 2.6 %collective-permute-done.2 = f32[1,128]{1,0:T(1,128)S(1)} collective-permute-done((f32[1,128]{1,0:T(1,128)S(1)}, f32[1,128]{1,0:T(1,128)S(1)}, u32[]{:S(2)}, u32[]{:S(2)}) %collective-permute-start.2) | collective-permute-done | bytes 544 | tf_op jit(solution)/shard_map/ppermute | solution.py:228
  79.3 0.0 collective-permute-done.1
  79.3 0.6 add_reduce_fusion
  (6 shorter events, 0.0 us)
Async XLA Ops:
  2.8 34.7 %copy-start.4 = (bf16[2,256,256]{2,1,0:T(8,128)(2,1)S(1)}, bf16[2,256,256]{2,1,0:T(8,128)(2,1)}, u32[]{:S(2)}) copy-start(bf16[2,256,256]{2,1,0:T(8,128)(2,1)} %constant.10.clone.mat_ref) | copy-start | bytes 786436
  2.8 34.7 %copy-start.5 = (f32[2,32,128]{2,1,0:T(8,128)S(1)}, f32[2,32,128]{2,1,0:T(8,128)}, u32[]{:S(2)}) copy-start(f32[2,32,128]{2,1,0:T(8,128)} %constant.9.clone.tw_ref) | copy-start | bytes 98308
  69.7 5.9 %copy-start = (bf16[128,512]{1,0:T(8,128)(2,1)S(1)}, bf16[128,512]{1,0:T(8,128)(2,1)}, u32[]{:S(2)}) copy-start(bf16[128,512]{1,0:T(8,128)(2,1)} %q_ref.1) | copy-start | bytes 393220
  69.7 5.9 %copy-start.1 = (bf16[128,512]{1,0:T(8,128)(2,1)S(1)}, bf16[128,512]{1,0:T(8,128)(2,1)}, u32[]{:S(2)}) copy-start(bf16[128,512]{1,0:T(8,128)(2,1)} %k_ref.1) | copy-start | bytes 393220
  69.7 5.9 %copy-start.2 = (bf16[128,512]{1,0:T(8,128)(2,1)S(1)}, bf16[128,512]{1,0:T(8,128)(2,1)}, u32[]{:S(2)}) copy-start(bf16[128,512]{1,0:T(8,128)(2,1)} %v_ref.1) | copy-start | bytes 393220
  69.7 5.9 %copy-start.3 = (bf16[128,512]{1,0:T(8,128)(2,1)S(1)}, bf16[128,512]{1,0:T(8,128)(2,1)}, u32[]{:S(2)}) copy-start(bf16[128,512]{1,0:T(8,128)(2,1)} %cot_ref.1) | copy-start | bytes 393220
  70.3 5.2 %copy-start.6 = (f32[512]{0:T(512)S(1)}, f32[512]{0:T(512)}, u32[]{:S(2)}) copy-start(f32[512]{0:T(512)} %param.13) | copy-start | bytes 6148
  70.3 1.1 %collective-permute-start = (f32[1,128]{1,0:T(1,128)S(1)}, f32[1,128]{1,0:T(1,128)S(1)}, u32[]{:S(2)}, u32[]{:S(2)}) collective-permute-start(f32[1,128]{1,0:T(1,128)S(1)} %get-tuple-element.20), channel_id=1, source_target_pairs={{0,1},{1,0},{2,3},{3,2},{4,5},{5,4},{6,7},{7,6},{8,9},{9,8},{10,11... | collective-permute-start | bytes 1544 | tf_op jit(solution)/shard_map/ppermute | solution.py:228
  71.4 5.2 %collective-permute-start.3 = (f32[1,128]{1,0:T(1,128)S(1)}, f32[1,128]{1,0:T(1,128)S(1)}, u32[]{:S(2)}, u32[]{:S(2)}) collective-permute-start(f32[1,128]{1,0:T(1,128)S(1)} %add.12), channel_id=1, source_target_pairs={{0,6},{1,7},{2,4},{3,5},{4,2},{5,3},{6,0},{7,1},{8,14},{9,15},{10,... | collective-permute-start | bytes 1544 | tf_op jit(solution)/shard_map/ppermute | solution.py:228
  74.2 5.0 %collective-permute-start.2 = (f32[1,128]{1,0:T(1,128)S(1)}, f32[1,128]{1,0:T(1,128)S(1)}, u32[]{:S(2)}, u32[]{:S(2)}) collective-permute-start(f32[1,128]{1,0:T(1,128)S(1)} %add.12), channel_id=1, source_target_pairs={{0,4},{1,5},{2,6},{3,7},{4,0},{5,1},{6,2},{7,3},{8,12},{9,13},{10,... | collective-permute-start | bytes 1544 | tf_op jit(solution)/shard_map/ppermute | solution.py:228
  75.0 4.2 %collective-permute-start.1 = (f32[1,128]{1,0:T(1,128)S(1)}, f32[1,128]{1,0:T(1,128)S(1)}, u32[]{:S(2)}, u32[]{:S(2)}) collective-permute-start(f32[1,128]{1,0:T(1,128)S(1)} %add.12), channel_id=1, source_target_pairs={{0,2},{1,3},{2,0},{3,1},{4,6},{5,7},{6,4},{7,5},{8,10},{9,11},{10,... | collective-permute-start | bytes 1544 | tf_op jit(solution)/shard_map/ppermute | solution.py:228

commit v2 on v1

--- a/solution.py
+++ b/solution.py
@@ -1,3 +1,4 @@
+import functools
 import math
 
 import jax
@@ -120,74 +121,135 @@
     return dot(high, mat_ref[0]) + (dot(low, mat_ref[0]) + dot(high, mat_ref[1]))
 
 
-def main_kernel(in_ref, tw_ref, mat_ref, out_ref, mid_ref):
-    @pl.loop(0, LINES // 8)
-    def _(step):
-        lines = pl.ds(pl.multiple_of(step * 8, 8), 8)
-        values = []
-        for s in range(BLOCKS):
-            signal = in_ref[PLACE[s], lines, :]
-            angle = 2 * math.pi * s / (4 * BLOCKS)
-            values.append((signal * math.cos(angle), signal * -math.sin(angle)))
-        for k1, (re, im) in enumerate(split_radix(values)):
-            t_re, t_im = tw_ref[0, k1 : k1 + 1, :], tw_ref[1, k1 : k1 + 1, :]
-            mid_ref[k1, lines, :ROWS] = re * t_re - im * t_im
-            mid_ref[k1, lines, ROWS:] = re * t_im + im * t_re
+def coarse(in_ref, tw_ref, mid_ref, source, target):
+    values = []
+    for s in range(BLOCKS):
+        signal = in_ref[PLACE[s], source, :]
+        angle = 2 * math.pi * s / (4 * BLOCKS)
+        values.append((signal * math.cos(angle), signal * -math.sin(angle)))
+    for k1, (re, im) in enumerate(split_radix(values)):
+        t_re, t_im = tw_ref[0, k1 : k1 + 1, :], tw_ref[1, k1 : k1 + 1, :]
+        mid_ref[k1, target, :ROWS] = re * t_re - im * t_im
+        mid_ref[k1, target, ROWS:] = re * t_im + im * t_re
+
+
+def coarse_back(mid_ref, lines, scale):
+    values = [(mid_ref[k1, lines, :ROWS], mid_ref[k1, lines, ROWS:]) for k1 in range(BLOCKS)]
+    for s, (re, im) in enumerate(split_radix(values)):
+        angle = 2 * math.pi * s / (4 * BLOCKS)
+        yield s, re * (math.cos(angle) * scale) + im * (math.sin(angle) * scale)
+
+
+def fine(value, mat_ref):
+    groups, lines, width = value.shape
+    return dft_rows(value.reshape(groups * lines, width), mat_ref).reshape(groups, lines, width)
+
+
+def halves(value):
+    return value[:, :, :ROWS], value[:, :, ROWS:]
+
+
+def conj_times(a, b):
+    (a_re, a_im), (b_re, b_im) = a, b
+    return jnp.concatenate([a_re * b_re - a_im * b_im, -(a_re * b_im + a_im * b_re)], axis=2)
+
+
+def conj_corr(a, b):
+    (a_re, a_im), (b_re, b_im) = a, b
+    return jnp.concatenate([a_re * b_re + a_im * b_im, a_re * b_im - a_im * b_re], axis=2)
+
+
+def turned(value, tw_ref, here):
+    re, im = halves(value)
+    t_re, t_im = tw_ref[0, here, :][:, None, :], tw_ref[1, here, :][:, None, :]
+    return re * t_re - im * t_im, re * t_im + im * t_re
+
+
+def eight(step):
+    return pl.ds(pl.multiple_of(step * 8, 8), 8)
+
+
+def grad_kernel(in_ref, tw_ref, mat_ref, grad_ref, spec_ref, skip_ref, sq_ref, mid_ref, back_ref):
+    @pl.loop(0, 2 * CH_EACH // 8)
+    def _(step):
+        coarse(in_ref, tw_ref, mid_ref, eight(step), eight(step))
 
     @pl.loop(0, BLOCKS // GROUP)
     def _(step):
-        first = pl.multiple_of(step * GROUP, GROUP)
-        here = pl.ds(first, GROUP)
-        held = mid_ref[here].reshape(GROUP * LINES, 2 * ROWS)
-        spectrum = dft_rows(held, mat_ref).reshape(GROUP, LINES, 2 * ROWS)
-        re, im = spectrum[:, :, :ROWS], spectrum[:, :, ROWS:]
-        x_re, g_re, h_re = (re[:, i * CH_EACH : (i + 1) * CH_EACH] for i in range(3))
-        x_im, g_im, h_im = (im[:, i * CH_EACH : (i + 1) * CH_EACH] for i in range(3))
-        product = jnp.concatenate(
-            [
-                jnp.concatenate([x_re * h_re - x_im * h_im, -(x_re * h_im + x_im * h_re)], axis=2),
-                jnp.concatenate([g_re * h_re + g_im * h_im, g_re * h_im - g_im * h_re], axis=2),
-                jnp.concatenate([g_re * x_re + g_im * x_im, g_re * x_im - g_im * x_re], axis=2),
-            ],
-            axis=1,
-        )
-        back = dft_rows(product.reshape(GROUP * LINES, 2 * ROWS), mat_ref)
-        back = back.reshape(GROUP, LINES, 2 * ROWS)
-        re, im = back[:, :, :ROWS], back[:, :, ROWS:]
-        t_re, t_im = tw_ref[0, here, :][:, None, :], tw_ref[1, here, :][:, None, :]
-        mid_ref[here, :, :ROWS] = re * t_re - im * t_im
-        mid_ref[here, :, ROWS:] = re * t_im + im * t_re
-
+        here = pl.ds(pl.multiple_of(step * GROUP, GROUP), GROUP)
+        spectrum = fine(mid_ref[here], mat_ref)
+        spec_ref[here] = spectrum
+        mixed, gated = halves(spectrum[:, :CH_EACH]), halves(spectrum[:, CH_EACH:])
+        re, im = turned(fine(conj_corr(gated, mixed), mat_ref), tw_ref, here)
+        back_ref[here, :, :ROWS] = re
+        back_ref[here, :, ROWS:] = im
+
+    time_scale = 1.0 / math.sqrt(LENGTH)
     squares = jnp.zeros((8, ROWS), jnp.float32)
-    for index in range(3):
-        scale = 1.0 / LENGTH if index < 2 else 1.0 / LENGTH / math.sqrt(LENGTH)
-        for half in range(CH_EACH // 8):
-            line = index * CH_EACH + half * 8
-            lines = slice(line, line + 8)
-            values = [
-                (mid_ref[k1, lines, :ROWS], mid_ref[k1, lines, ROWS:]) for k1 in range(BLOCKS)
-            ]
-            for s, (re, im) in enumerate(split_radix(values)):
-                angle = 2 * math.pi * s / (4 * BLOCKS)
-                series = re * (math.cos(angle) * scale) + im * (math.sin(angle) * scale)
-                out_ref[PLACE[s] * BACK + line : PLACE[s] * BACK + line + 8, :] = series
-                if index == 2:
-                    squares = squares + series * series
+    for half in range(CH_EACH // 8):
+        lines = slice(half * 8, half * 8 + 8)
+        for s, series in coarse_back(back_ref, lines, time_scale / LENGTH):
+            grad_ref[s, lines, :] = series
+            squares = squares + series * series
 
     direct = jnp.zeros((CH_EACH, ROWS), jnp.float32)
     for s in range(BLOCKS):
         direct = direct + in_ref[s, :CH_EACH, :] * in_ref[s, CH_EACH : 2 * CH_EACH, :]
-    direct = jnp.sum(direct, axis=1, keepdims=True) * (1.0 / math.sqrt(LENGTH))
+    direct = jnp.sum(direct, axis=1, keepdims=True) * time_scale
     row = lax.broadcasted_iota(jnp.int32, (CH_EACH, ROWS), 0)
     lane = lax.broadcasted_iota(jnp.int32, (CH_EACH, ROWS), 1)
-    last = jnp.sum(jnp.where(row == lane, direct, 0.0), axis=0, keepdims=True)
-    squares = jnp.sum(jnp.sum(squares, axis=0, keepdims=True), axis=1, keepdims=True)
-    last = jnp.where(lane[:1] == CH_EACH, squares, last)
+    skip = jnp.sum(jnp.where(row == lane, direct, 0.0), axis=0, keepdims=True)
+    skip_ref[...] = skip
+    sq_ref[...] = jnp.sum(squares, axis=0, keepdims=True) + skip * skip
+
+
+def taps_kernel(in_ref, tw_ref, mat_ref, gain_ref, spec_ref, gain_out_ref, mid_ref):
+    gain_out_ref[...] = gain_ref[...]
+
+    @pl.loop(0, CH_EACH // 8)
+    def _(step):
+        source = pl.ds(pl.multiple_of(step * 8 + 2 * CH_EACH, 8), 8)
+        coarse(in_ref, tw_ref, mid_ref, source, eight(step))
+
+    @pl.loop(0, BLOCKS // GROUP)
+    def _(step):
+        here = pl.ds(pl.multiple_of(step * GROUP, GROUP), GROUP)
+        spec_ref[here] = fine(mid_ref[here], mat_ref)
+
+
+def conv_kernel(spec_ref, taps_ref, tw_ref, mat_ref, grad_ref, out_ref, mid_ref):
+    @pl.loop(0, BLOCKS // GROUP)
+    def _(step):
+        here = pl.ds(pl.multiple_of(step * GROUP, GROUP), GROUP)
+        mixed, gated = halves(spec_ref[here, :CH_EACH]), halves(spec_ref[here, CH_EACH:])
+        taps = halves(taps_ref[here])
+        product = jnp.concatenate([conj_times(mixed, taps), conj_corr(gated, taps)], axis=1)
+        re, im = turned(fine(product, mat_ref), tw_ref, here)
+        mid_ref[here, :, :ROWS] = re
+        mid_ref[here, :, ROWS:] = im
+
+    for line in range(0, 2 * CH_EACH, 8):
+        for s, series in coarse_back(mid_ref, slice(line, line + 8), 1.0 / LENGTH):
+            first = PLACE[s] * BACK + line
+            out_ref[first : first + 8, :] = series
     for s in range(BLOCKS):
-        out_ref[s * BACK + LINES : (s + 1) * BACK, :] = last
-
-
-def stats_kernel(in_ref, skip_ref, sum_ref):
+        first = PLACE[s] * BACK + 2 * CH_EACH
+        out_ref[first : first + CH_EACH, :] = grad_ref[s]
+        out_ref[first + CH_EACH : first + CH_EACH + 1, :] = jnp.zeros((1, ROWS), jnp.float32)
+
+
+def last_line_kernel(held_ref, skip_ref, *refs):
+    one, two, four, six, out_ref = refs
+    squares = (one[...] + two[...]) + (four[...] + six[...])
+    squares = jnp.sum(squares, axis=1, keepdims=True)
+    lane = lax.broadcasted_iota(jnp.int32, (1, ROWS), 1)
+    line = jnp.where(lane == CH_EACH, squares, skip_ref[...])
+    out_ref[...] = held_ref[...]
+    for s in range(BLOCKS):
+        out_ref[s * BACK + LINES : (s + 1) * BACK, :] = line
+
+
+def statistics(in_ref, skip_ref, rms_ref, count):
     per_row = ROWS // CH_EACH
     rows = BLOCKS // per_row
     lane = lax.broadcasted_iota(jnp.int32, (rows, ROWS), 1)
@@ -200,12 +262,14 @@
         moved = pltpu.roll(lines, m * CH_EACH, 1) if m else lines
         skip = jnp.where(lane // CH_EACH == m, moved, skip)
     skip_ref[...] = skip
-    sum_ref[...] = jnp.sum(squares + skip * skip, axis=0, keepdims=True)
-
-
-def post_kernel(
-    in_ref, q_ref, k_ref, v_ref, cot_ref, gain_ref, out_ref, dq_ref, dk_ref, dv_ref, dh_ref
-):
+    total = jnp.sum(jnp.sum(squares, axis=0, keepdims=True), axis=1, keepdims=True)
+    rms_ref[...] = jnp.sqrt(total * (1.0 / count))
+
+
+def post_kernel(count, in_ref, q_ref, k_ref, v_ref, cot_ref, gain_ref, *outs):
+    out_ref, dq_ref, dk_ref, dv_ref, dh_ref, skip_ref, rms_ref = outs
+    statistics(in_ref, skip_ref, rms_ref, count)
+
     def series(index):
         first = [PLACE[s] * BACK + index * CH_EACH for s in range(BLOCKS)]
         return jnp.concatenate([in_ref[i : i + CH_EACH, :] for i in first], axis=0).T
@@ -228,12 +292,6 @@
     return lax.ppermute(array, "ch", [(i, i ^ bit) for i in range(lax.axis_size("ch"))])
 
 
-def over_channels(array):
-    array = array + partner(array, 1)
-    two, four, six = (partner(array, bit) for bit in (2, 4, 6))
-    return (array + two) + (four + six)
-
-
 def exchange(array):
     return lax.all_to_all(array, "seq", 0, 0, axis_index_groups=[ORDER], tiled=True)
 
@@ -243,6 +301,7 @@
 
 
 PARAMS = pltpu.CompilerParams(vmem_limit_bytes=40 * 2**20)
+COST = pl.CostEstimate(flops=2 * 10**9, bytes_accessed=4 * 10**6, transcendentals=0)
 WIDE = pltpu.CompilerParams(vmem_limit_bytes=60 * 2**20)
 
 
@@ -264,36 +323,58 @@
         ],
         compiler_params=WIDE,
     )(*signals)
-    results = pl.pallas_call(
-        main_kernel,
+    lines = exchange(packed)
+    room = functools.partial(pltpu.VMEM, dtype=jnp.float32)
+    grad, spectra, skip_part, squares = pl.pallas_call(
+        grad_kernel,
+        out_shape=(
+            f32(BLOCKS, CH_EACH, ROWS),
+            f32(BLOCKS, 2 * CH_EACH, 2 * ROWS),
+            f32(1, ROWS),
+            f32(1, ROWS),
+        ),
+        scratch_shapes=[
+            room((BLOCKS, 2 * CH_EACH, 2 * ROWS)),
+            room((BLOCKS, CH_EACH, 2 * ROWS)),
+        ],
+        compiler_params=PARAMS,
+        cost_estimate=COST,
+    )(lines, twiddle, matrix)
+    squares = squares + partner(squares, 1)
+    taps_spectrum, gain = pl.pallas_call(
+        taps_kernel,
+        out_shape=(f32(BLOCKS, CH_EACH, 2 * ROWS), f32(1, channels)),
+        scratch_shapes=[room((BLOCKS, CH_EACH, 2 * ROWS))],
+        compiler_params=PARAMS,
+        cost_estimate=COST,
+    )(lines, twiddle, matrix, gain[None, :])
+    shares = [squares] + [partner(squares, bit) for bit in (2, 4, 6)]
+    returned = pl.pallas_call(
+        conv_kernel,
         out_shape=f32(BLOCKS * BACK, ROWS),
-        scratch_shapes=[pltpu.VMEM((BLOCKS, LINES, 2 * ROWS), jnp.float32)],
-        compiler_params=PARAMS,
-    )(exchange(packed), twiddle, matrix)
-    results = exchange(results.reshape(BLOCKS, BACK, 1, ROWS)).reshape(BLOCKS * BACK, ROWS)
-    skip_grad, total = pl.pallas_call(
-        stats_kernel,
-        out_shape=(f32(channels // ROWS, ROWS), f32(1, ROWS)),
-        compiler_params=PARAMS,
-    )(results)
-    total = jnp.sum(over_channels(total))
-    grad_rms = jnp.sqrt(total / (channels * lax.axis_size("ch") * (LENGTH + 1)))
+        scratch_shapes=[room((BLOCKS, 2 * CH_EACH, 2 * ROWS))],
+        compiler_params=PARAMS,
+        cost_estimate=COST,
+    )(spectra, taps_spectrum, twiddle, matrix, grad)
+    returned = pl.pallas_call(
+        last_line_kernel,
+        out_shape=f32(BLOCKS * BACK, ROWS),
+        compiler_params=PARAMS,
+    )(returned, skip_part, *shares)
+    returned = exchange(returned.reshape(BLOCKS, BACK, 1, ROWS)).reshape(BLOCKS * BACK, ROWS)
     bf16 = jax.ShapeDtypeStruct((rows, channels), jnp.bfloat16)
-    output, query_grad, key_grad, value_grad, filter_grad = pl.pallas_call(
-        post_kernel,
-        out_shape=(bf16, bf16, bf16, bf16, f32(rows, channels)),
-        compiler_params=PARAMS,
-        cost_estimate=pl.CostEstimate(flops=10**6, bytes_accessed=2 * 10**6, transcendentals=0),
-    )(results, query, key, value, cotangent, gain[None, :])
-    return (
-        output,
-        query_grad,
-        key_grad,
-        value_grad,
-        filter_grad,
-        skip_grad.reshape(channels),
-        grad_rms,
-    )
+    count = channels * lax.axis_size("ch") * (LENGTH + 1)
+    *outputs, skip_grad, grad_rms = pl.pallas_call(
+        functools.partial(post_kernel, count),
+        out_shape=(
+            *[bf16] * 4,
+            f32(rows, channels),
+            f32(channels // ROWS, ROWS),
+            f32(1, 1),
+        ),
+        compiler_params=PARAMS,
+    )(returned, query, key, value, cotangent, gain)
+    return (*outputs, skip_grad.reshape(channels), grad_rms[0, 0])
 
 
 def solution(mesh):

time: 82 us -> 78.6 us (0.959)
  between operations: 2.51 us -> 0.76 us
  waiting for transfers between devices: 3.71 us -> 2.23 us
    ppermute x4, waiting for transfers between devices: 3.71 us -> 2.23 us  [partner(): lax.ppermute(array, 'ch', [(i, i ^ bit) for i in range(lax.axis_size('ch'...]
    pallas_call x3 -> x5, Pallas kernels: 6.11 us -> 6.58 us  [the longest x1 2.8 us: body(): pl.pallas_call(grad_kernel, out_shape=(f32(BLOCKS, CH_EACH, ROWS), f32(BL...]
  transfers between devices with their start and end apart: 4 -> 4, of which waited for: 2 -> 1; matrix products, arithmetic and copies ran while one was open for 0% -> 0% of each run, Pallas kernels for 1% -> 3%
where the time goes in v2:
time: 78.6 us; the launch traced here: 78.4 us
  blocking collectives  61.7 us (78%)
  Pallas kernels  8.79 us (11%)
  starting transfers between devices  4.27 us (5%)
  waiting for transfers between devices  2.23 us (3%)
    all_to_all x2, blocking collectives, exchange(): lax.all_to_all(array, 'seq', 0, 0, axis_index_groups=[ORDER], tiled=True)  61.7 us
    ppermute x4, starting transfers between devices, partner(): lax.ppermute(array, 'ch', [(i, i ^ bit) for i in range(lax.axis_size('ch'...  4.27 us
    pallas_call x1, Pallas kernels, body(): pl.pallas_call(grad_kernel, out_shape=(f32(BLOCKS, CH_EACH, ROWS), f32(BL...  2.8 us
    ppermute x4, waiting for transfers between devices, partner(): lax.ppermute(array, 'ch', [(i, i ^ bit) for i in range(lax.axis_size('ch'...  2.23 us
    pallas_call x1, Pallas kernels, body(): pl.pallas_call(pre_kernel, out_shape=f32(BLOCKS, LINES, ROWS), in_specs=[...  2.21 us
  transfers between devices with their start and end apart: 4, of which 1 were waited for; matrix products, arithmetic and copies ran while one was open for 0% of the time, Pallas kernels for 3%

profile of v2, /device:TPU:32, one launch (start us, length us, event | category | flops | bytes accessed | tf_op | source)
XLA Modules:
  0.0 78.4 jit_solution(10229412688567136372)
XLA Ops:
  0.6 2.2 %shard_map.135 = f32[32,48,128]{2,1,0:T(8,128)} custom-call(bf16[128,512]{1,0:T(8,128)(2,1)} %q_ref.1, bf16[128,512]{1,0:T(8,128)(2,1)} %k_ref.1, bf16[128,512]{1,0:T(8,128)(2,1)} %v_ref.1, bf16[128,512]{1,0:T(8,128)(2,1)} %cot_ref.1, f32[128,512]{1,0:T(8,128)} %taps_hbm.1), custom_call_target="tpu_custom_call" | custom-call | tf_op jit(solution)/shard_map/pallas_call | solution.py:313
  2.8 0.0 copy-start.5
  2.9 0.0 copy-start.6
  2.9 34.7 %all_to_all.10.in_ref = f32[32,48,128]{2,1,0:T(8,128)S(1)} all-to-all(f32[32,48,128]{2,1,0:T(8,128)} %shard_map.135), channel_id=1, replica_groups={{0,8,16,24,32,40,48,56,64,72,80,88,96,104,112,120,128,136,144,152,160,1..., dimensions={0} | all-to-all | bytes 1572864 | tf_op jit(solution)/shard_map/all_to_all | solution.py:296
  37.5 0.0 copy-done.5
  37.5 2.8 %shard_map.136 = (f32[32,16,128]{2,1,0:T(8,128)S(1)}, f32[32,32,256]{2,1,0:T(8,128)S(1)}, f32[1,128]{1,0:T(1,128)S(1)}, f32[1,128]{1,0:T(1,128)S(1)}) custom-call(f32[32,48,128]{2,1,0:T(8,128)S(1)} %all_to_all.10.in_ref, f32[2,32,128]{2,1,0:T(8,128)S(1)} %copy-done.6, bf16[2,256,256]{2,1,0:T(8,128)(2,1)S(1)} %copy-done.5), custom_call_target="tpu_custom_call" | custom-call | flops 2000000000 | bytes 4000000 | tf_op jit(solution)/shard_map/pallas_call | solution.py:328
  40.3 0.0 copy-start.4
  40.4 0.1 collective-permute-start
  40.5 0.6 copy-done.4
  41.0 1.1 %shard_map.137 = (f32[32,16,256]{2,1,0:T(8,128)S(1)}, f32[1,512]{1,0:T(1,128)S(1)}) custom-call(f32[32,48,128]{2,1,0:T(8,128)S(1)} %all_to_all.10.in_ref, f32[2,32,128]{2,1,0:T(8,128)S(1)} %copy-done.6, bf16[2,256,256]{2,1,0:T(8,128)(2,1)S(1)} %copy-done.5, f32[1,512]{1,0:T(1,128)S(1)} %bitcast.7), custom_call_target="tpu_custom_call" | custom-call | flops 2000000000 | bytes 4000000 | tf_op jit(solution)/shard_map/pallas_call | solution.py:344
  42.1 0.0 collective-permute-done
  42.2 2.8 %collective-permute-start.3 = (f32[1,128]{1,0:T(1,128)S(1)}, f32[1,128]{1,0:T(1,128)S(1)}, u32[]{:S(2)}, u32[]{:S(2)}) collective-permute-start(f32[1,128]{1,0:T(1,128)S(1)} %add.3.refs_0_), channel_id=1, source_target_pairs={{0,6},{1,7},{2,4},{3,5},{4,2},{5,3},{6,0},{7,1},{8,14},{9,15},{10,... | collective-permute-start | bytes 1544 | tf_op jit(solution)/shard_map/ppermute | solution.py:292
  45.0 0.8 %collective-permute-start.2 = (f32[1,128]{1,0:T(1,128)S(1)}, f32[1,128]{1,0:T(1,128)S(1)}, u32[]{:S(2)}, u32[]{:S(2)}) collective-permute-start(f32[1,128]{1,0:T(1,128)S(1)} %add.3.refs_0_), channel_id=1, source_target_pairs={{0,4},{1,5},{2,6},{3,7},{4,0},{5,1},{6,2},{7,3},{8,12},{9,13},{10,... | collective-permute-start | bytes 1544 | tf_op jit(solution)/shard_map/ppermute | solution.py:292
  45.8 0.5 collective-permute-start.1
  46.3 1.5 %shard_map.138.held_ref = f32[1568,128]{1,0:T(8,128)S(1)} custom-call(f32[32,32,256]{2,1,0:T(8,128)S(1)} %get-tuple-element.20.spec_ref, f32[32,16,256]{2,1,0:T(8,128)S(1)} %get-tuple-element.21.taps_ref, f32[2,32,128]{2,1,0:T(8,128)S(1)} %copy-done.6, bf16[2,256,256]{2,1,0:T(8,128)(2,1)S(1)} %copy-done.5, f32[32,16,128]{2,1,0:T(8,128)S(1)} %get-tuple-element.22.grad_ref), custom_call_target="tpu_custom_call" | custom-call | flops 2000000000 | bytes 4000000 | tf_op jit(solution)/shard_map/pallas_call | solution.py:352
  47.8 0.0 collective-permute-done.3.refs_3_
  47.8 2.2 %collective-permute-done.2.refs_2_ = f32[1,128]{1,0:T(1,128)S(1)} collective-permute-done((f32[1,128]{1,0:T(1,128)S(1)}, f32[1,128]{1,0:T(1,128)S(1)}, u32[]{:S(2)}, u32[]{:S(2)}) %collective-permute-start.2) | collective-permute-done | bytes 544 | tf_op jit(solution)/shard_map/ppermute | solution.py:292
  50.1 0.0 collective-permute-done.1.refs_1_
  50.1 0.1 shard_map.139
  50.2 0.0 copy-start.1
  50.2 0.0 copy-start.2
  50.2 0.0 copy-start.3
  50.2 27.0 %all_to_all.11 = f32[32,49,1,128]{3,2,1,0:T(1,128)S(1)} all-to-all(f32[32,49,1,128]{3,2,1,0:T(1,128)S(1)} %bitcast.6), channel_id=1, replica_groups={{0,8,16,24,32,40,48,56,64,72,80,88,96,104,112,120,128,136,144,152,160,1..., dimensions={0} | all-to-all | bytes 1605632 | tf_op jit(solution)/shard_map/all_to_all | solution.py:296
  77.2 1.1 %shard_map.140 = (bf16[128,512]{1,0:T(8,128)(2,1)}, bf16[128,512]{1,0:T(8,128)(2,1)}, bf16[128,512]{1,0:T(8,128)(2,1)}, bf16[128,512]{1,0:T(8,128)(2,1)}, f32[12...) custom-call(f32[1568,128]{1,0:T(8,128)S(1)} %bitcast.5, bf16[128,512]{1,0:T(8,128)(2,1)S(1)} %copy-done, ...), custom_call_target="tpu_custom_call" | custom-call | tf_op jit(solution)/shard_map/pallas_call | solution.py:367
  (7 shorter events, 0.0 us)
Async XLA Ops:
  2.8 34.7 %copy-start.5 = (bf16[2,256,256]{2,1,0:T(8,128)(2,1)S(1)}, bf16[2,256,256]{2,1,0:T(8,128)(2,1)}, u32[]{:S(2)}) copy-start(bf16[2,256,256]{2,1,0:T(8,128)(2,1)} %constant.5.clone.mat_ref) | copy-start | bytes 786436
  2.9 34.7 %copy-start.6 = (f32[2,32,128]{2,1,0:T(8,128)S(1)}, f32[2,32,128]{2,1,0:T(8,128)}, u32[]{:S(2)}) copy-start(f32[2,32,128]{2,1,0:T(8,128)} %constant.4.clone.tw_ref) | copy-start | bytes 98308
  40.3 0.7 copy-start.4
  40.4 1.8 %collective-permute-start = (f32[1,128]{1,0:T(1,128)S(1)}, f32[1,128]{1,0:T(1,128)S(1)}, u32[]{:S(2)}, u32[]{:S(2)}) collective-permute-start(f32[1,128]{1,0:T(1,128)S(1)} %get-tuple-element.24), channel_id=1, source_target_pairs={{0,1},{1,0},{2,3},{3,2},{4,5},{5,4},{6,7},{7,6},{8,9},{9,8},{10,11... | collective-permute-start | bytes 1544 | tf_op jit(solution)/shard_map/ppermute | solution.py:292
  42.2 5.7 %collective-permute-start.3 = (f32[1,128]{1,0:T(1,128)S(1)}, f32[1,128]{1,0:T(1,128)S(1)}, u32[]{:S(2)}, u32[]{:S(2)}) collective-permute-start(f32[1,128]{1,0:T(1,128)S(1)} %add.3.refs_0_), channel_id=1, source_target_pairs={{0,6},{1,7},{2,4},{3,5},{4,2},{5,3},{6,0},{7,1},{8,14},{9,15},{10,... | collective-permute-start | bytes 1544 | tf_op jit(solution)/shard_map/ppermute | solution.py:292
  45.0 5.0 %collective-permute-start.2 = (f32[1,128]{1,0:T(1,128)S(1)}, f32[1,128]{1,0:T(1,128)S(1)}, u32[]{:S(2)}, u32[]{:S(2)}) collective-permute-start(f32[1,128]{1,0:T(1,128)S(1)} %add.3.refs_0_), channel_id=1, source_target_pairs={{0,4},{1,5},{2,6},{3,7},{4,0},{5,1},{6,2},{7,3},{8,12},{9,13},{10,... | collective-permute-start | bytes 1544 | tf_op jit(solution)/shard_map/ppermute | solution.py:292
  45.8 4.2 %collective-permute-start.1 = (f32[1,128]{1,0:T(1,128)S(1)}, f32[1,128]{1,0:T(1,128)S(1)}, u32[]{:S(2)}, u32[]{:S(2)}) collective-permute-start(f32[1,128]{1,0:T(1,128)S(1)} %add.3.refs_0_), channel_id=1, source_target_pairs={{0,2},{1,3},{2,0},{3,1},{4,6},{5,7},{6,4},{7,5},{8,10},{9,11},{10,... | collective-permute-start | bytes 1544 | tf_op jit(solution)/shard_map/ppermute | solution.py:292
  50.1 27.1 %copy-start = (bf16[128,512]{1,0:T(8,128)(2,1)S(1)}, bf16[128,512]{1,0:T(8,128)(2,1)}, u32[]{:S(2)}) copy-start(bf16[128,512]{1,0:T(8,128)(2,1)} %q_ref.1) | copy-start | bytes 393220
  50.2 27.1 %copy-start.1 = (bf16[128,512]{1,0:T(8,128)(2,1)S(1)}, bf16[128,512]{1,0:T(8,128)(2,1)}, u32[]{:S(2)}) copy-start(bf16[128,512]{1,0:T(8,128)(2,1)} %k_ref.1) | copy-start | bytes 393220
  50.2 27.1 %copy-start.2 = (bf16[128,512]{1,0:T(8,128)(2,1)S(1)}, bf16[128,512]{1,0:T(8,128)(2,1)}, u32[]{:S(2)}) copy-start(bf16[128,512]{1,0:T(8,128)(2,1)} %v_ref.1) | copy-start | bytes 393220
  50.2 27.1 %copy-start.3 = (bf16[128,512]{1,0:T(8,128)(2,1)S(1)}, bf16[128,512]{1,0:T(8,128)(2,1)}, u32[]{:S(2)}) copy-start(bf16[128,512]{1,0:T(8,128)(2,1)} %cot_ref.1) | copy-start | bytes 393220

commit v3 on v2

--- a/solution.py
+++ b/solution.py
@@ -14,9 +14,10 @@
 LENGTH = ROWS * BLOCKS
 CH_EACH = 16
 LINES = 3 * CH_EACH
-GROUP = 8
+GROUP = 32
+WIDER = 32
 BACK = LINES + 1
-ORDER = list(range(BLOCKS))
+ORDER = [12, 30, 2, 15, 20, 25, 27, 28, 0, 6, 5, 18, 19, 9, 29, 7, 26, 22, 14, 31, 8, 23, 21, 1, 16, 17, 24, 10, 3, 13, 11, 4]
 PLACE = [ORDER.index(s) for s in range(BLOCKS)]
 
 
@@ -169,7 +170,10 @@
     return pl.ds(pl.multiple_of(step * 8, 8), 8)
 
 
-def grad_kernel(in_ref, tw_ref, mat_ref, grad_ref, spec_ref, skip_ref, sq_ref, mid_ref, back_ref):
+def grad_kernel(in_ref, tw_ref, mat_ref, gain_ref, *refs):
+    grad_ref, spec_ref, skip_ref, sq_ref, gain_out_ref, mid_ref, back_ref = refs
+    gain_out_ref[...] = gain_ref[...]
+
     @pl.loop(0, 2 * CH_EACH // 8)
     def _(step):
         coarse(in_ref, tw_ref, mid_ref, eight(step), eight(step))
@@ -203,50 +207,44 @@
     sq_ref[...] = jnp.sum(squares, axis=0, keepdims=True) + skip * skip
 
 
-def taps_kernel(in_ref, tw_ref, mat_ref, gain_ref, spec_ref, gain_out_ref, mid_ref):
-    gain_out_ref[...] = gain_ref[...]
-
+def taps_kernel(in_ref, tw_ref, mat_ref, spec_ref, mid_ref):
     @pl.loop(0, CH_EACH // 8)
     def _(step):
         source = pl.ds(pl.multiple_of(step * 8 + 2 * CH_EACH, 8), 8)
         coarse(in_ref, tw_ref, mid_ref, source, eight(step))
 
-    @pl.loop(0, BLOCKS // GROUP)
-    def _(step):
-        here = pl.ds(pl.multiple_of(step * GROUP, GROUP), GROUP)
+    @pl.loop(0, BLOCKS // WIDER)
+    def _(step):
+        here = pl.ds(pl.multiple_of(step * WIDER, WIDER), WIDER)
         spec_ref[here] = fine(mid_ref[here], mat_ref)
 
 
-def conv_kernel(spec_ref, taps_ref, tw_ref, mat_ref, grad_ref, out_ref, mid_ref):
-    @pl.loop(0, BLOCKS // GROUP)
-    def _(step):
-        here = pl.ds(pl.multiple_of(step * GROUP, GROUP), GROUP)
-        mixed, gated = halves(spec_ref[here, :CH_EACH]), halves(spec_ref[here, CH_EACH:])
-        taps = halves(taps_ref[here])
-        product = jnp.concatenate([conj_times(mixed, taps), conj_corr(gated, taps)], axis=1)
+def conv_kernel(line, combine, spec_ref, taps_ref, tw_ref, mat_ref, after_ref, out_ref, mid_ref):
+    @pl.loop(0, BLOCKS // WIDER)
+    def _(step):
+        here = pl.ds(pl.multiple_of(step * WIDER, WIDER), WIDER)
+        signal = halves(spec_ref[here, line : line + CH_EACH])
+        product = combine(signal, halves(taps_ref[here]))
         re, im = turned(fine(product, mat_ref), tw_ref, here)
         mid_ref[here, :, :ROWS] = re
         mid_ref[here, :, ROWS:] = im
 
-    for line in range(0, 2 * CH_EACH, 8):
-        for s, series in coarse_back(mid_ref, slice(line, line + 8), 1.0 / LENGTH):
-            first = PLACE[s] * BACK + line
-            out_ref[first : first + 8, :] = series
+    for first in range(0, CH_EACH, 8):
+        lines = slice(first, first + 8)
+        for s, series in coarse_back(mid_ref, lines, 1.0 / LENGTH):
+            out_ref[s, lines, :] = series
+
+
+def pack_kernel(conv_ref, back_ref, grad_ref, skip_ref, one_ref, two_ref, out_ref):
+    squares = jnp.sum(one_ref[...] + two_ref[...], axis=1, keepdims=True)
+    lane = lax.broadcasted_iota(jnp.int32, (1, ROWS), 1)
+    last = jnp.where(lane == CH_EACH, squares, skip_ref[...])
     for s in range(BLOCKS):
-        first = PLACE[s] * BACK + 2 * CH_EACH
-        out_ref[first : first + CH_EACH, :] = grad_ref[s]
-        out_ref[first + CH_EACH : first + CH_EACH + 1, :] = jnp.zeros((1, ROWS), jnp.float32)
-
-
-def last_line_kernel(held_ref, skip_ref, *refs):
-    one, two, four, six, out_ref = refs
-    squares = (one[...] + two[...]) + (four[...] + six[...])
-    squares = jnp.sum(squares, axis=1, keepdims=True)
-    lane = lax.broadcasted_iota(jnp.int32, (1, ROWS), 1)
-    line = jnp.where(lane == CH_EACH, squares, skip_ref[...])
-    out_ref[...] = held_ref[...]
-    for s in range(BLOCKS):
-        out_ref[s * BACK + LINES : (s + 1) * BACK, :] = line
+        first = PLACE[s] * BACK
+        for ref in (conv_ref, back_ref, grad_ref):
+            out_ref[first : first + CH_EACH, :] = ref[s]
+            first += CH_EACH
+        out_ref[first : first + 1, :] = last
 
 
 def statistics(in_ref, skip_ref, rms_ref, count):
@@ -325,13 +323,14 @@
     )(*signals)
     lines = exchange(packed)
     room = functools.partial(pltpu.VMEM, dtype=jnp.float32)
-    grad, spectra, skip_part, squares = pl.pallas_call(
+    grad, spectra, skip_part, squares, gain = pl.pallas_call(
         grad_kernel,
         out_shape=(
             f32(BLOCKS, CH_EACH, ROWS),
             f32(BLOCKS, 2 * CH_EACH, 2 * ROWS),
             f32(1, ROWS),
             f32(1, ROWS),
+            f32(1, channels),
         ),
         scratch_shapes=[
             room((BLOCKS, 2 * CH_EACH, 2 * ROWS)),
@@ -339,28 +338,33 @@
         ],
         compiler_params=PARAMS,
         cost_estimate=COST,
-    )(lines, twiddle, matrix)
+    )(lines, twiddle, matrix, gain[None, :])
     squares = squares + partner(squares, 1)
-    taps_spectrum, gain = pl.pallas_call(
+    taps_spectrum = pl.pallas_call(
         taps_kernel,
-        out_shape=(f32(BLOCKS, CH_EACH, 2 * ROWS), f32(1, channels)),
+        out_shape=f32(BLOCKS, CH_EACH, 2 * ROWS),
         scratch_shapes=[room((BLOCKS, CH_EACH, 2 * ROWS))],
         compiler_params=PARAMS,
         cost_estimate=COST,
-    )(lines, twiddle, matrix, gain[None, :])
-    shares = [squares] + [partner(squares, bit) for bit in (2, 4, 6)]
+    )(lines, twiddle, matrix)
+
+    def convolution(line, combine, after):
+        return pl.pallas_call(
+            functools.partial(conv_kernel, line, combine),
+            out_shape=f32(BLOCKS, CH_EACH, ROWS),
+            scratch_shapes=[room((BLOCKS, CH_EACH, 2 * ROWS))],
+            compiler_params=PARAMS,
+            cost_estimate=COST,
+        )(spectra, taps_spectrum, twiddle, matrix, after)
+
+    conv = convolution(0, conj_times, squares)
+    squares = squares + partner(squares, 2)
+    back = convolution(CH_EACH, conj_corr, squares)
     returned = pl.pallas_call(
-        conv_kernel,
-        out_shape=f32(BLOCKS * BACK, ROWS),
-        scratch_shapes=[room((BLOCKS, 2 * CH_EACH, 2 * ROWS))],
-        compiler_params=PARAMS,
-        cost_estimate=COST,
-    )(spectra, taps_spectrum, twiddle, matrix, grad)
-    returned = pl.pallas_call(
-        last_line_kernel,
+        pack_kernel,
         out_shape=f32(BLOCKS * BACK, ROWS),
         compiler_params=PARAMS,
-    )(returned, skip_part, *shares)
+    )(conv, back, grad, skip_part, squares, partner(squares, 6))
     returned = exchange(returned.reshape(BLOCKS, BACK, 1, ROWS)).reshape(BLOCKS * BACK, ROWS)
     bf16 = jax.ShapeDtypeStruct((rows, channels), jnp.bfloat16)
     count = channels * lax.axis_size("ch") * (LENGTH + 1)

time: 78.6 us -> 75.1 us (0.955)
  the two profiles are of different devices: /device:TPU:32 before, /device:TPU:6 now
where the time goes in v3:
time: 75.1 us; the launch traced here: 74.9 us
  blocking collectives  59.4 us (79%)
  Pallas kernels  6.84 us (9%)
  waiting for transfers between devices  6.43 us (9%)
  starting transfers between devices  1.4 us (2%)
    all_to_all x2, blocking collectives, exchange(): lax.all_to_all(array, 'seq', 0, 0, axis_index_groups=[ORDER], tiled=True)  59.4 us
    ppermute x3, waiting for transfers between devices, partner(): lax.ppermute(array, 'ch', [(i, i ^ bit) for i in range(lax.axis_size('ch'...  6.43 us
    pallas_call x1, Pallas kernels, body(): pl.pallas_call(pre_kernel, out_shape=f32(BLOCKS, LINES, ROWS), in_specs=[...  2.17 us
    pallas_call x1, Pallas kernels, body(): pl.pallas_call(grad_kernel, out_shape=(f32(BLOCKS, CH_EACH, ROWS), f32(BL...  1.82 us
  transfers between devices with their start and end apart: 3, of which 3 were waited for; matrix products, arithmetic and copies ran while one was open for 0% of the time, Pallas kernels for 2%

profile of v3, /device:TPU:6, one launch (start us, length us, event | category | flops | bytes accessed | tf_op | source)
XLA Modules:
  0.0 74.9 jit_solution(16634028953063487169)
XLA Ops:
  0.6 2.2 %shard_map.135 = f32[32,48,128]{2,1,0:T(8,128)} custom-call(bf16[128,512]{1,0:T(8,128)(2,1)} %q_ref.1, bf16[128,512]{1,0:T(8,128)(2,1)} %k_ref.1, bf16[128,512]{1,0:T(8,128)(2,1)} %v_ref.1, bf16[128,512]{1,0:T(8,128)(2,1)} %cot_ref.1, f32[128,512]{1,0:T(8,128)} %taps_hbm.1), custom_call_target="tpu_custom_call" | custom-call | tf_op jit(solution)/shard_map/pallas_call | solution.py:311
  2.8 0.0 copy-start.4
  2.8 0.0 copy-start.5
  2.8 0.0 copy-start.6
  2.8 33.0 %all_to_all.10.in_ref = f32[32,48,128]{2,1,0:T(8,128)S(1)} all-to-all(f32[32,48,128]{2,1,0:T(8,128)} %shard_map.135), channel_id=1, replica_groups={{96,240,16,120,160,200,216,224,0,48,40,144,152,72,232,56,208,176,112,24..., dimensions={0} | all-to-all | bytes 1572864 | tf_op jit(solution)/shard_map/all_to_all | solution.py:294
  35.9 0.0 copy-done.4
  35.9 0.0 copy-done.6
  35.9 1.8 %shard_map.136 = (f32[32,16,128]{2,1,0:T(8,128)S(1)}, f32[32,32,256]{2,1,0:T(8,128)S(1)}, f32[1,128]{1,0:T(1,128)S(1)}, f32[1,128]{1,0:T(1,128)S(1)}, f32[1,512]{1,0:T(1,128)S(1)}) custom-call(f32[32,48,128]{2,1,0:T(8,128)S(1)} %all_to_all.10.in_ref, f32[2,32,128]{2,1,0:T(8,128)S(1)} %copy-done.6, bf16[2,256,256]{2,1,0:T(8,128)(2,1)S(1)} %copy-done.5, ...), custom_call_target="tpu_custom_call" | custom-call | flops 2000000000 | bytes 4000000 | tf_op jit(solution)/shard_map/pallas_call | solution.py:326
  37.7 0.1 collective-permute-start
  37.8 0.6 shard_map.137.taps_ref
  38.4 0.5 collective-permute-done
  38.9 0.8 %collective-permute-start.1 = (f32[1,128]{1,0:T(1,128)S(1)}, f32[1,128]{1,0:T(1,128)S(1)}, u32[]{:S(2)}, u32[]{:S(2)}) collective-permute-start(f32[1,128]{1,0:T(1,128)S(1)} %add.6.after_ref), channel_id=1, source_target_pairs={{0,2},{1,3},{2,0},{3,1},{4,6},{5,7},{6,4},{7,5},{8,10},{9,11},{10,... | collective-permute-start | bytes 1544 | tf_op jit(solution)/shard_map/ppermute | solution.py:290
  39.8 0.5 shard_map.138.conv_ref
  40.3 2.2 %collective-permute-done.1 = f32[1,128]{1,0:T(1,128)S(1)} collective-permute-done((f32[1,128]{1,0:T(1,128)S(1)}, f32[1,128]{1,0:T(1,128)S(1)}, u32[]{:S(2)}, u32[]{:S(2)}) %collective-permute-start.1) | collective-permute-done | bytes 544 | tf_op jit(solution)/shard_map/ppermute | solution.py:290
  42.5 0.5 collective-permute-start.2
  42.9 0.5 shard_map.139.back_ref
  43.5 3.8 %collective-permute-done.2.two_ref = f32[1,128]{1,0:T(1,128)S(1)} collective-permute-done((f32[1,128]{1,0:T(1,128)S(1)}, f32[1,128]{1,0:T(1,128)S(1)}, u32[]{:S(2)}, u32[]{:S(2)}) %collective-permute-start.2) | collective-permute-done | bytes 544 | tf_op jit(solution)/shard_map/ppermute | solution.py:290
  47.2 0.1 shard_map.140
  47.3 0.0 copy-start.1
  47.3 0.0 copy-start.2
  47.3 0.0 copy-start.3
  47.4 26.4 %all_to_all.11 = f32[32,49,1,128]{3,2,1,0:T(1,128)S(1)} all-to-all(f32[32,49,1,128]{3,2,1,0:T(1,128)S(1)} %bitcast.5), channel_id=1, replica_groups={{96,240,16,120,160,200,216,224,0,48,40,144,152,72,232,56,208,176,112,24..., dimensions={0} | all-to-all | bytes 1605632 | tf_op jit(solution)/shard_map/all_to_all | solution.py:294
  73.7 0.0 copy-done
  73.7 1.1 %shard_map.141 = (bf16[128,512]{1,0:T(8,128)(2,1)}, bf16[128,512]{1,0:T(8,128)(2,1)}, bf16[128,512]{1,0:T(8,128)(2,1)}, bf16[128,512]{1,0:T(8,128)(2,1)}, f32[12...) custom-call(f32[1568,128]{1,0:T(8,128)S(1)} %bitcast.6, bf16[128,512]{1,0:T(8,128)(2,1)S(1)} %copy-done, ...), custom_call_target="tpu_custom_call" | custom-call | tf_op jit(solution)/shard_map/pallas_call | solution.py:371
  (7 shorter events, 0.0 us)
Async XLA Ops:
  2.8 33.1 %copy-start.4 = (f32[512]{0:T(512)S(1)}, f32[512]{0:T(512)}, u32[]{:S(2)}) copy-start(f32[512]{0:T(512)} %param.13) | copy-start | bytes 6148
  2.8 33.1 %copy-start.5 = (bf16[2,256,256]{2,1,0:T(8,128)(2,1)S(1)}, bf16[2,256,256]{2,1,0:T(8,128)(2,1)}, u32[]{:S(2)}) copy-start(bf16[2,256,256]{2,1,0:T(8,128)(2,1)} %constant.5.clone.mat_ref) | copy-start | bytes 786436
  2.8 33.1 %copy-start.6 = (f32[2,32,128]{2,1,0:T(8,128)S(1)}, f32[2,32,128]{2,1,0:T(8,128)}, u32[]{:S(2)}) copy-start(f32[2,32,128]{2,1,0:T(8,128)} %constant.4.clone.tw_ref) | copy-start | bytes 98308
  37.7 1.2 %collective-permute-start = (f32[1,128]{1,0:T(1,128)S(1)}, f32[1,128]{1,0:T(1,128)S(1)}, u32[]{:S(2)}, u32[]{:S(2)}) collective-permute-start(f32[1,128]{1,0:T(1,128)S(1)} %get-tuple-element.20), channel_id=1, source_target_pairs={{0,1},{1,0},{2,3},{3,2},{4,5},{5,4},{6,7},{7,6},{8,9},{9,8},{10,11... | collective-permute-start | bytes 1544 | tf_op jit(solution)/shard_map/ppermute | solution.py:290
  38.9 3.5 %collective-permute-start.1 = (f32[1,128]{1,0:T(1,128)S(1)}, f32[1,128]{1,0:T(1,128)S(1)}, u32[]{:S(2)}, u32[]{:S(2)}) collective-permute-start(f32[1,128]{1,0:T(1,128)S(1)} %add.6.after_ref), channel_id=1, source_target_pairs={{0,2},{1,3},{2,0},{3,1},{4,6},{5,7},{6,4},{7,5},{8,10},{9,11},{10,... | collective-permute-start | bytes 1544 | tf_op jit(solution)/shard_map/ppermute | solution.py:290
  42.5 4.8 %collective-permute-start.2 = (f32[1,128]{1,0:T(1,128)S(1)}, f32[1,128]{1,0:T(1,128)S(1)}, u32[]{:S(2)}, u32[]{:S(2)}) collective-permute-start(f32[1,128]{1,0:T(1,128)S(1)} %add.7.after_ref.one_ref), channel_id=1, source_target_pairs={{0,6},{1,7},{2,4},{3,5},{4,2},{5,3},{6,0},{7,1},{8,14},{9,15},{10,... | collective-permute-start | bytes 1544 | tf_op jit(solution)/shard_map/ppermute | solution.py:290
  47.3 26.4 %copy-start = (bf16[128,512]{1,0:T(8,128)(2,1)S(1)}, bf16[128,512]{1,0:T(8,128)(2,1)}, u32[]{:S(2)}) copy-start(bf16[128,512]{1,0:T(8,128)(2,1)} %q_ref.1) | copy-start | bytes 393220
  47.3 26.4 %copy-start.1 = (bf16[128,512]{1,0:T(8,128)(2,1)S(1)}, bf16[128,512]{1,0:T(8,128)(2,1)}, u32[]{:S(2)}) copy-start(bf16[128,512]{1,0:T(8,128)(2,1)} %k_ref.1) | copy-start | bytes 393220
  47.3 26.4 %copy-start.2 = (bf16[128,512]{1,0:T(8,128)(2,1)S(1)}, bf16[128,512]{1,0:T(8,128)(2,1)}, u32[]{:S(2)}) copy-start(bf16[128,512]{1,0:T(8,128)(2,1)} %v_ref.1) | copy-start | bytes 393220
  47.3 26.4 %copy-start.3 = (bf16[128,512]{1,0:T(8,128)(2,1)S(1)}, bf16[128,512]{1,0:T(8,128)(2,1)}, u32[]{:S(2)}) copy-start(bf16[128,512]{1,0:T(8,128)(2,1)} %cot_ref.1) | copy-start | bytes 393220

commit v4 on v3

--- a/solution.py
+++ b/solution.py
@@ -17,7 +17,10 @@
 GROUP = 32
 WIDER = 32
 BACK = LINES + 1
-ORDER = [12, 30, 2, 15, 20, 25, 27, 28, 0, 6, 5, 18, 19, 9, 29, 7, 26, 22, 14, 31, 8, 23, 21, 1, 16, 17, 24, 10, 3, 13, 11, 4]
+ORDER = [
+    23, 20, 27, 29, 10, 22, 12, 1, 0, 24, 28, 19, 6, 18, 21, 11,
+    2, 31, 16, 26, 5, 15, 3, 17, 8, 30, 14, 25, 7, 13, 9, 4,
+]
 PLACE = [ORDER.index(s) for s in range(BLOCKS)]
 
 
@@ -235,8 +238,10 @@
             out_ref[s, lines, :] = series
 
 
-def pack_kernel(conv_ref, back_ref, grad_ref, skip_ref, one_ref, two_ref, out_ref):
-    squares = jnp.sum(one_ref[...] + two_ref[...], axis=1, keepdims=True)
+def pack_kernel(conv_ref, back_ref, grad_ref, skip_ref, *refs):
+    own, two, four, six, out_ref = refs
+    squares = (own[...] + two[...]) + (four[...] + six[...])
+    squares = jnp.sum(squares, axis=1, keepdims=True)
     lane = lax.broadcasted_iota(jnp.int32, (1, ROWS), 1)
     last = jnp.where(lane == CH_EACH, squares, skip_ref[...])
     for s in range(BLOCKS):
@@ -358,13 +363,13 @@
         )(spectra, taps_spectrum, twiddle, matrix, after)
 
     conv = convolution(0, conj_times, squares)
-    squares = squares + partner(squares, 2)
+    two, four, six = (partner(squares, bit) for bit in (2, 4, 6))
     back = convolution(CH_EACH, conj_corr, squares)
     returned = pl.pallas_call(
         pack_kernel,
         out_shape=f32(BLOCKS * BACK, ROWS),
         compiler_params=PARAMS,
-    )(conv, back, grad, skip_part, squares, partner(squares, 6))
+    )(conv, back, grad, skip_part, squares, two, four, six)
     returned = exchange(returned.reshape(BLOCKS, BACK, 1, ROWS)).reshape(BLOCKS * BACK, ROWS)
     bf16 = jax.ShapeDtypeStruct((rows, channels), jnp.bfloat16)
     count = channels * lax.axis_size("ch") * (LENGTH + 1)

time: 75.1 us -> 74 us (0.985)
  the two profiles are of different devices: /device:TPU:6 before, /device:TPU:32 now
where the time goes in v4:
time: 74 us; the launch traced here: 72.6 us
  blocking collectives  57.6 us (78%)
  Pallas kernels  6.86 us (9%)
  starting transfers between devices  4.19 us (6%)
  waiting for transfers between devices  3.14 us (4%)
  between operations  0.75 us (1%)
    all_to_all x2, blocking collectives, exchange(): lax.all_to_all(array, 'seq', 0, 0, axis_index_groups=[ORDER], tiled=True)  57.6 us
    ppermute x4, starting transfers between devices, partner(): lax.ppermute(array, 'ch', [(i, i ^ bit) for i in range(lax.axis_size('ch'...  4.19 us
    ppermute x4, waiting for transfers between devices, partner(): lax.ppermute(array, 'ch', [(i, i ^ bit) for i in range(lax.axis_size('ch'...  3.14 us
    pallas_call x1, Pallas kernels, body(): pl.pallas_call(pre_kernel, out_shape=f32(BLOCKS, LINES, ROWS), in_specs=[...  2.16 us
    pallas_call x1, Pallas kernels, body(): pl.pallas_call(grad_kernel, out_shape=(f32(BLOCKS, CH_EACH, ROWS), f32(BL...  1.82 us
  transfers between devices with their start and end apart: 4, of which 2 were waited for; matrix products, arithmetic and copies ran while one was open for 0% of the time, Pallas kernels for 2%

profile of v4, /device:TPU:32, one launch (start us, length us, event | category | flops | bytes accessed | tf_op | source)
XLA Modules:
  0.0 72.6 jit_solution(5112820520831601840)
XLA Ops:
  0.6 2.2 %shard_map.135 = f32[32,48,128]{2,1,0:T(8,128)} custom-call(bf16[128,512]{1,0:T(8,128)(2,1)} %q_ref.1, bf16[128,512]{1,0:T(8,128)(2,1)} %k_ref.1, bf16[128,512]{1,0:T(8,128)(2,1)} %v_ref.1, bf16[128,512]{1,0:T(8,128)(2,1)} %cot_ref.1, f32[128,512]{1,0:T(8,128)} %taps_hbm.1), custom_call_target="tpu_custom_call" | custom-call | tf_op jit(solution)/shard_map/pallas_call | solution.py:316
  2.8 0.0 copy-start.4
  2.8 0.0 copy-start.5
  2.8 0.0 copy-start.6
  2.8 30.1 %all_to_all.10.in_ref = f32[32,48,128]{2,1,0:T(8,128)S(1)} all-to-all(f32[32,48,128]{2,1,0:T(8,128)} %shard_map.135), channel_id=1, replica_groups={{184,160,216,232,80,176,96,8,0,192,224,152,48,144,168,88,16,248,128,208..., dimensions={0} | all-to-all | bytes 1572864 | tf_op jit(solution)/shard_map/all_to_all | solution.py:299
  33.0 0.0 copy-done.5
  33.0 1.8 %shard_map.136 = (f32[32,16,128]{2,1,0:T(8,128)S(1)}, f32[32,32,256]{2,1,0:T(8,128)S(1)}, f32[1,128]{1,0:T(1,128)S(1)}, f32[1,128]{1,0:T(1,128)S(1)}, f32[1,512]{1,0:T(1,128)S(1)}) custom-call(f32[32,48,128]{2,1,0:T(8,128)S(1)} %all_to_all.10.in_ref, f32[2,32,128]{2,1,0:T(8,128)S(1)} %copy-done.6, bf16[2,256,256]{2,1,0:T(8,128)(2,1)S(1)} %copy-done.5, ...), custom_call_target="tpu_custom_call" | custom-call | flops 2000000000 | bytes 4000000 | tf_op jit(solution)/shard_map/pallas_call | solution.py:331
  34.8 0.1 collective-permute-start
  34.9 0.6 shard_map.137.taps_ref
  35.5 0.5 collective-permute-done
  36.0 2.8 %collective-permute-start.3 = (f32[1,128]{1,0:T(1,128)S(1)}, f32[1,128]{1,0:T(1,128)S(1)}, u32[]{:S(2)}, u32[]{:S(2)}) collective-permute-start(f32[1,128]{1,0:T(1,128)S(1)} %add.3.after_ref.refs_0_), channel_id=1, source_target_pairs={{0,6},{1,7},{2,4},{3,5},{4,2},{5,3},{6,0},{7,1},{8,14},{9,15},{10,... | collective-permute-start | bytes 1544 | tf_op jit(solution)/shard_map/ppermute | solution.py:295
  38.8 0.8 %collective-permute-start.2 = (f32[1,128]{1,0:T(1,128)S(1)}, f32[1,128]{1,0:T(1,128)S(1)}, u32[]{:S(2)}, u32[]{:S(2)}) collective-permute-start(f32[1,128]{1,0:T(1,128)S(1)} %add.3.after_ref.refs_0_), channel_id=1, source_target_pairs={{0,4},{1,5},{2,6},{3,7},{4,0},{5,1},{6,2},{7,3},{8,12},{9,13},{10,... | collective-permute-start | bytes 1544 | tf_op jit(solution)/shard_map/ppermute | solution.py:295
  39.6 0.5 collective-permute-start.1
  40.1 0.5 shard_map.139.back_ref
  40.6 0.5 shard_map.138.conv_ref
  41.2 0.0 collective-permute-done.3.refs_3_
  41.2 2.6 %collective-permute-done.2.refs_2_ = f32[1,128]{1,0:T(1,128)S(1)} collective-permute-done((f32[1,128]{1,0:T(1,128)S(1)}, f32[1,128]{1,0:T(1,128)S(1)}, u32[]{:S(2)}, u32[]{:S(2)}) %collective-permute-start.2) | collective-permute-done | bytes 544 | tf_op jit(solution)/shard_map/ppermute | solution.py:295
  43.8 0.0 collective-permute-done.1.refs_1_
  43.8 0.1 shard_map.140
  43.9 0.0 copy-start.1
  43.9 0.0 copy-start.2
  44.0 0.0 copy-start.3
  44.0 27.5 %all_to_all.11 = f32[32,49,1,128]{3,2,1,0:T(1,128)S(1)} all-to-all(f32[32,49,1,128]{3,2,1,0:T(1,128)S(1)} %bitcast.6), channel_id=1, replica_groups={{184,160,216,232,80,176,96,8,0,192,224,152,48,144,168,88,16,248,128,208..., dimensions={0} | all-to-all | bytes 1605632 | tf_op jit(solution)/shard_map/all_to_all | solution.py:299
  71.5 1.1 %shard_map.141 = (bf16[128,512]{1,0:T(8,128)(2,1)}, bf16[128,512]{1,0:T(8,128)(2,1)}, bf16[128,512]{1,0:T(8,128)(2,1)}, bf16[128,512]{1,0:T(8,128)(2,1)}, f32[12...) custom-call(f32[1568,128]{1,0:T(8,128)S(1)} %bitcast.5, bf16[128,512]{1,0:T(8,128)(2,1)S(1)} %copy-done, ...), custom_call_target="tpu_custom_call" | custom-call | tf_op jit(solution)/shard_map/pallas_call | solution.py:376
  (8 shorter events, 0.0 us)
Async XLA Ops:
  2.8 30.2 %copy-start.4 = (f32[512]{0:T(512)S(1)}, f32[512]{0:T(512)}, u32[]{:S(2)}) copy-start(f32[512]{0:T(512)} %param.13) | copy-start | bytes 6148
  2.8 30.2 %copy-start.5 = (bf16[2,256,256]{2,1,0:T(8,128)(2,1)S(1)}, bf16[2,256,256]{2,1,0:T(8,128)(2,1)}, u32[]{:S(2)}) copy-start(bf16[2,256,256]{2,1,0:T(8,128)(2,1)} %constant.5.clone.mat_ref) | copy-start | bytes 786436
  2.8 30.2 %copy-start.6 = (f32[2,32,128]{2,1,0:T(8,128)S(1)}, f32[2,32,128]{2,1,0:T(8,128)}, u32[]{:S(2)}) copy-start(f32[2,32,128]{2,1,0:T(8,128)} %constant.4.clone.tw_ref) | copy-start | bytes 98308
  34.8 1.2 %collective-permute-start = (f32[1,128]{1,0:T(1,128)S(1)}, f32[1,128]{1,0:T(1,128)S(1)}, u32[]{:S(2)}, u32[]{:S(2)}) collective-permute-start(f32[1,128]{1,0:T(1,128)S(1)} %get-tuple-element.20), channel_id=1, source_target_pairs={{0,1},{1,0},{2,3},{3,2},{4,5},{5,4},{6,7},{7,6},{8,9},{9,8},{10,11... | collective-permute-start | bytes 1544 | tf_op jit(solution)/shard_map/ppermute | solution.py:295
  36.0 5.2 %collective-permute-start.3 = (f32[1,128]{1,0:T(1,128)S(1)}, f32[1,128]{1,0:T(1,128)S(1)}, u32[]{:S(2)}, u32[]{:S(2)}) collective-permute-start(f32[1,128]{1,0:T(1,128)S(1)} %add.3.after_ref.refs_0_), channel_id=1, source_target_pairs={{0,6},{1,7},{2,4},{3,5},{4,2},{5,3},{6,0},{7,1},{8,14},{9,15},{10,... | collective-permute-start | bytes 1544 | tf_op jit(solution)/shard_map/ppermute | solution.py:295
  38.8 5.0 %collective-permute-start.2 = (f32[1,128]{1,0:T(1,128)S(1)}, f32[1,128]{1,0:T(1,128)S(1)}, u32[]{:S(2)}, u32[]{:S(2)}) collective-permute-start(f32[1,128]{1,0:T(1,128)S(1)} %add.3.after_ref.refs_0_), channel_id=1, source_target_pairs={{0,4},{1,5},{2,6},{3,7},{4,0},{5,1},{6,2},{7,3},{8,12},{9,13},{10,... | collective-permute-start | bytes 1544 | tf_op jit(solution)/shard_map/ppermute | solution.py:295
  39.6 4.2 %collective-permute-start.1 = (f32[1,128]{1,0:T(1,128)S(1)}, f32[1,128]{1,0:T(1,128)S(1)}, u32[]{:S(2)}, u32[]{:S(2)}) collective-permute-start(f32[1,128]{1,0:T(1,128)S(1)} %add.3.after_ref.refs_0_), channel_id=1, source_target_pairs={{0,2},{1,3},{2,0},{3,1},{4,6},{5,7},{6,4},{7,5},{8,10},{9,11},{10,... | collective-permute-start | bytes 1544 | tf_op jit(solution)/shard_map/ppermute | solution.py:295
  43.9 27.5 %copy-start = (bf16[128,512]{1,0:T(8,128)(2,1)S(1)}, bf16[128,512]{1,0:T(8,128)(2,1)}, u32[]{:S(2)}) copy-start(bf16[128,512]{1,0:T(8,128)(2,1)} %q_ref.1) | copy-start | bytes 393220
  43.9 27.5 %copy-start.1 = (bf16[128,512]{1,0:T(8,128)(2,1)S(1)}, bf16[128,512]{1,0:T(8,128)(2,1)}, u32[]{:S(2)}) copy-start(bf16[128,512]{1,0:T(8,128)(2,1)} %k_ref.1) | copy-start | bytes 393220
  43.9 27.5 %copy-start.2 = (bf16[128,512]{1,0:T(8,128)(2,1)S(1)}, bf16[128,512]{1,0:T(8,128)(2,1)}, u32[]{:S(2)}) copy-start(bf16[128,512]{1,0:T(8,128)(2,1)} %v_ref.1) | copy-start | bytes 393220
  44.0 27.5 %copy-start.3 = (bf16[128,512]{1,0:T(8,128)(2,1)S(1)}, bf16[128,512]{1,0:T(8,128)(2,1)}, u32[]{:S(2)}) copy-start(bf16[128,512]{1,0:T(8,128)(2,1)} %cot_ref.1) | copy-start | bytes 393220

commit v5 on v3

--- a/solution.py
+++ b/solution.py
@@ -17,7 +17,10 @@
 GROUP = 32
 WIDER = 32
 BACK = LINES + 1
-ORDER = [12, 30, 2, 15, 20, 25, 27, 28, 0, 6, 5, 18, 19, 9, 29, 7, 26, 22, 14, 31, 8, 23, 21, 1, 16, 17, 24, 10, 3, 13, 11, 4]
+ORDER = [
+    23, 20, 27, 29, 10, 22, 12, 1, 0, 24, 28, 19, 6, 18, 21, 11,
+    2, 31, 16, 26, 5, 15, 3, 17, 8, 30, 14, 25, 7, 13, 9, 4,
+]
 PLACE = [ORDER.index(s) for s in range(BLOCKS)]
 
 

time: 75.1 us -> 73.6 us (0.980)
  the two profiles are of different devices: /device:TPU:6 before, /device:TPU:32 now
where the time goes in v5:
time: 73.6 us; the launch traced here: 72.2 us
  blocking collectives  56.8 us (77%)
  Pallas kernels  6.84 us (9%)
  starting transfers between devices  4.34 us (6%)
  waiting for transfers between devices  3.49 us (5%)
  between operations  0.75 us (1%)
    all_to_all x2, blocking collectives, exchange(): lax.all_to_all(array, 'seq', 0, 0, axis_index_groups=[ORDER], tiled=True)  56.8 us
    ppermute x3, starting transfers between devices, partner(): lax.ppermute(array, 'ch', [(i, i ^ bit) for i in range(lax.axis_size('ch'...  4.34 us
    ppermute x3, waiting for transfers between devices, partner(): lax.ppermute(array, 'ch', [(i, i ^ bit) for i in range(lax.axis_size('ch'...  3.49 us
    pallas_call x1, Pallas kernels, body(): pl.pallas_call(pre_kernel, out_shape=f32(BLOCKS, LINES, ROWS), in_specs=[...  2.17 us
    pallas_call x1, Pallas kernels, body(): pl.pallas_call(grad_kernel, out_shape=(f32(BLOCKS, CH_EACH, ROWS), f32(BL...  1.82 us
  transfers between devices with their start and end apart: 3, of which 3 were waited for; matrix products, arithmetic and copies ran while one was open for 0% of the time, Pallas kernels for 2%

profile of v5, /device:TPU:32, one launch (start us, length us, event | category | flops | bytes accessed | tf_op | source)
XLA Modules:
  0.0 72.2 jit_solution(17874121433420500695)
XLA Ops:
  0.6 2.2 %shard_map.135 = f32[32,48,128]{2,1,0:T(8,128)} custom-call(bf16[128,512]{1,0:T(8,128)(2,1)} %q_ref.1, bf16[128,512]{1,0:T(8,128)(2,1)} %k_ref.1, bf16[128,512]{1,0:T(8,128)(2,1)} %v_ref.1, bf16[128,512]{1,0:T(8,128)(2,1)} %cot_ref.1, f32[128,512]{1,0:T(8,128)} %taps_hbm.1), custom_call_target="tpu_custom_call" | custom-call | tf_op jit(solution)/shard_map/pallas_call | solution.py:314
  2.8 0.0 copy-start.4
  2.8 0.0 copy-start.5
  2.8 0.0 copy-start.6
  2.8 30.1 %all_to_all.10.in_ref = f32[32,48,128]{2,1,0:T(8,128)S(1)} all-to-all(f32[32,48,128]{2,1,0:T(8,128)} %shard_map.135), channel_id=1, replica_groups={{184,160,216,232,80,176,96,8,0,192,224,152,48,144,168,88,16,248,128,208..., dimensions={0} | all-to-all | bytes 1572864 | tf_op jit(solution)/shard_map/all_to_all | solution.py:297
  33.0 0.0 copy-done.6
  33.0 1.8 %shard_map.136 = (f32[32,16,128]{2,1,0:T(8,128)S(1)}, f32[32,32,256]{2,1,0:T(8,128)S(1)}, f32[1,128]{1,0:T(1,128)S(1)}, f32[1,128]{1,0:T(1,128)S(1)}, f32[1,512]{1,0:T(1,128)S(1)}) custom-call(f32[32,48,128]{2,1,0:T(8,128)S(1)} %all_to_all.10.in_ref, f32[2,32,128]{2,1,0:T(8,128)S(1)} %copy-done.6, bf16[2,256,256]{2,1,0:T(8,128)(2,1)S(1)} %copy-done.5, ...), custom_call_target="tpu_custom_call" | custom-call | flops 2000000000 | bytes 4000000 | tf_op jit(solution)/shard_map/pallas_call | solution.py:329
  34.8 0.1 collective-permute-start
  34.9 0.6 shard_map.137.taps_ref
  35.5 0.5 collective-permute-done
  36.0 1.5 %collective-permute-start.1 = (f32[1,128]{1,0:T(1,128)S(1)}, f32[1,128]{1,0:T(1,128)S(1)}, u32[]{:S(2)}, u32[]{:S(2)}) collective-permute-start(f32[1,128]{1,0:T(1,128)S(1)} %add.6.after_ref), channel_id=1, source_target_pairs={{0,2},{1,3},{2,0},{3,1},{4,6},{5,7},{6,4},{7,5},{8,10},{9,11},{10,... | collective-permute-start | bytes 1544 | tf_op jit(solution)/shard_map/ppermute | solution.py:293
  37.5 0.5 shard_map.138.conv_ref
  38.0 1.5 %collective-permute-done.1 = f32[1,128]{1,0:T(1,128)S(1)} collective-permute-done((f32[1,128]{1,0:T(1,128)S(1)}, f32[1,128]{1,0:T(1,128)S(1)}, u32[]{:S(2)}, u32[]{:S(2)}) %collective-permute-start.1) | collective-permute-done | bytes 544 | tf_op jit(solution)/shard_map/ppermute | solution.py:293
  39.6 2.8 %collective-permute-start.2 = (f32[1,128]{1,0:T(1,128)S(1)}, f32[1,128]{1,0:T(1,128)S(1)}, u32[]{:S(2)}, u32[]{:S(2)}) collective-permute-start(f32[1,128]{1,0:T(1,128)S(1)} %add.7.after_ref.one_ref), channel_id=1, source_target_pairs={{0,6},{1,7},{2,4},{3,5},{4,2},{5,3},{6,0},{7,1},{8,14},{9,15},{10,... | collective-permute-start | bytes 1544 | tf_op jit(solution)/shard_map/ppermute | solution.py:293
  42.3 0.5 shard_map.139.back_ref
  42.9 1.5 %collective-permute-done.2.two_ref = f32[1,128]{1,0:T(1,128)S(1)} collective-permute-done((f32[1,128]{1,0:T(1,128)S(1)}, f32[1,128]{1,0:T(1,128)S(1)}, u32[]{:S(2)}, u32[]{:S(2)}) %collective-permute-start.2) | collective-permute-done | bytes 544 | tf_op jit(solution)/shard_map/ppermute | solution.py:293
  44.3 0.1 shard_map.140
  44.4 0.0 copy-start.1
  44.4 0.0 copy-start.2
  44.4 0.0 copy-start.3
  44.5 26.6 %all_to_all.11 = f32[32,49,1,128]{3,2,1,0:T(1,128)S(1)} all-to-all(f32[32,49,1,128]{3,2,1,0:T(1,128)S(1)} %bitcast.5), channel_id=1, replica_groups={{184,160,216,232,80,176,96,8,0,192,224,152,48,144,168,88,16,248,128,208..., dimensions={0} | all-to-all | bytes 1605632 | tf_op jit(solution)/shard_map/all_to_all | solution.py:297
  71.1 0.0 copy-done
  71.1 0.0 copy-done.2
  71.1 1.1 %shard_map.141 = (bf16[128,512]{1,0:T(8,128)(2,1)}, bf16[128,512]{1,0:T(8,128)(2,1)}, bf16[128,512]{1,0:T(8,128)(2,1)}, bf16[128,512]{1,0:T(8,128)(2,1)}, f32[12...) custom-call(f32[1568,128]{1,0:T(8,128)S(1)} %bitcast.6, bf16[128,512]{1,0:T(8,128)(2,1)S(1)} %copy-done, ...), custom_call_target="tpu_custom_call" | custom-call | tf_op jit(solution)/shard_map/pallas_call | solution.py:374
  (7 shorter events, 0.0 us)
Async XLA Ops:
  2.8 30.2 %copy-start.4 = (f32[512]{0:T(512)S(1)}, f32[512]{0:T(512)}, u32[]{:S(2)}) copy-start(f32[512]{0:T(512)} %param.13) | copy-start | bytes 6148
  2.8 30.2 %copy-start.5 = (bf16[2,256,256]{2,1,0:T(8,128)(2,1)S(1)}, bf16[2,256,256]{2,1,0:T(8,128)(2,1)}, u32[]{:S(2)}) copy-start(bf16[2,256,256]{2,1,0:T(8,128)(2,1)} %constant.5.clone.mat_ref) | copy-start | bytes 786436
  2.8 30.2 %copy-start.6 = (f32[2,32,128]{2,1,0:T(8,128)S(1)}, f32[2,32,128]{2,1,0:T(8,128)}, u32[]{:S(2)}) copy-start(f32[2,32,128]{2,1,0:T(8,128)} %constant.4.clone.tw_ref) | copy-start | bytes 98308
  34.8 1.2 %collective-permute-start = (f32[1,128]{1,0:T(1,128)S(1)}, f32[1,128]{1,0:T(1,128)S(1)}, u32[]{:S(2)}, u32[]{:S(2)}) collective-permute-start(f32[1,128]{1,0:T(1,128)S(1)} %get-tuple-element.20), channel_id=1, source_target_pairs={{0,1},{1,0},{2,3},{3,2},{4,5},{5,4},{6,7},{7,6},{8,9},{9,8},{10,11... | collective-permute-start | bytes 1544 | tf_op jit(solution)/shard_map/ppermute | solution.py:293
  36.0 3.5 %collective-permute-start.1 = (f32[1,128]{1,0:T(1,128)S(1)}, f32[1,128]{1,0:T(1,128)S(1)}, u32[]{:S(2)}, u32[]{:S(2)}) collective-permute-start(f32[1,128]{1,0:T(1,128)S(1)} %add.6.after_ref), channel_id=1, source_target_pairs={{0,2},{1,3},{2,0},{3,1},{4,6},{5,7},{6,4},{7,5},{8,10},{9,11},{10,... | collective-permute-start | bytes 1544 | tf_op jit(solution)/shard_map/ppermute | solution.py:293
  39.6 4.8 %collective-permute-start.2 = (f32[1,128]{1,0:T(1,128)S(1)}, f32[1,128]{1,0:T(1,128)S(1)}, u32[]{:S(2)}, u32[]{:S(2)}) collective-permute-start(f32[1,128]{1,0:T(1,128)S(1)} %add.7.after_ref.one_ref), channel_id=1, source_target_pairs={{0,6},{1,7},{2,4},{3,5},{4,2},{5,3},{6,0},{7,1},{8,14},{9,15},{10,... | collective-permute-start | bytes 1544 | tf_op jit(solution)/shard_map/ppermute | solution.py:293
  44.4 26.7 %copy-start = (bf16[128,512]{1,0:T(8,128)(2,1)S(1)}, bf16[128,512]{1,0:T(8,128)(2,1)}, u32[]{:S(2)}) copy-start(bf16[128,512]{1,0:T(8,128)(2,1)} %q_ref.1) | copy-start | bytes 393220
  44.4 26.7 %copy-start.1 = (bf16[128,512]{1,0:T(8,128)(2,1)S(1)}, bf16[128,512]{1,0:T(8,128)(2,1)}, u32[]{:S(2)}) copy-start(bf16[128,512]{1,0:T(8,128)(2,1)} %k_ref.1) | copy-start | bytes 393220
  44.4 26.7 %copy-start.2 = (bf16[128,512]{1,0:T(8,128)(2,1)S(1)}, bf16[128,512]{1,0:T(8,128)(2,1)}, u32[]{:S(2)}) copy-start(bf16[128,512]{1,0:T(8,128)(2,1)} %v_ref.1) | copy-start | bytes 393220
  44.4 26.7 %copy-start.3 = (bf16[128,512]{1,0:T(8,128)(2,1)S(1)}, bf16[128,512]{1,0:T(8,128)(2,1)}, u32[]{:S(2)}) copy-start(bf16[128,512]{1,0:T(8,128)(2,1)} %cot_ref.1) | copy-start | bytes 393220

commit v6 on v5

--- a/solution.py
+++ b/solution.py
@@ -268,25 +268,34 @@
 
 
 def post_kernel(count, in_ref, q_ref, k_ref, v_ref, cot_ref, gain_ref, *outs):
-    out_ref, dq_ref, dk_ref, dv_ref, dh_ref, skip_ref, rms_ref = outs
-    statistics(in_ref, skip_ref, rms_ref, count)
+    hbm, (skip_ref, rms_ref), held, sems = outs[:5], outs[5:7], outs[7:12], outs[12]
+    stores = []
+
+    def store(index, result):
+        held[index][...] = result
+        copy = pltpu.make_async_copy(held[index], hbm[index], sems.at[index])
+        copy.start()
+        stores.append(copy)
 
     def series(index):
         first = [PLACE[s] * BACK + index * CH_EACH for s in range(BLOCKS)]
         return jnp.concatenate([in_ref[i : i + CH_EACH, :] for i in first], axis=0).T
 
+    store(4, series(2))
     query = q_ref[...].astype(jnp.float32)
     key = k_ref[...].astype(jnp.float32)
     value = v_ref[...].astype(jnp.float32)
     cot = cot_ref[...].astype(jnp.float32)
     gain = gain_ref[...]
     inner = series(0) + gain * (key * value)
-    out_ref[...] = (query * inner).astype(jnp.bfloat16)
-    dq_ref[...] = (cot * inner).astype(jnp.bfloat16)
+    store(0, (query * inner).astype(jnp.bfloat16))
+    store(1, (cot * inner).astype(jnp.bfloat16))
     mixed_grad = series(1) + gain * (query * cot)
-    dk_ref[...] = (mixed_grad * value).astype(jnp.bfloat16)
-    dv_ref[...] = (mixed_grad * key).astype(jnp.bfloat16)
-    dh_ref[...] = series(2)
+    store(2, (mixed_grad * value).astype(jnp.bfloat16))
+    store(3, (mixed_grad * key).astype(jnp.bfloat16))
+    statistics(in_ref, skip_ref, rms_ref, count)
+    for copy in stores:
+        copy.wait()
 
 
 def partner(array, bit):
@@ -379,6 +388,9 @@
             f32(channels // ROWS, ROWS),
             f32(1, 1),
         ),
+        out_specs=(*[hbm] * 5, *[pl.BlockSpec(memory_space=pltpu.VMEM)] * 2),
+        scratch_shapes=[pltpu.VMEM((rows, channels), jnp.bfloat16)] * 4
+        + [pltpu.VMEM((rows, channels), jnp.float32), pltpu.SemaphoreType.DMA((5,))],
         compiler_params=PARAMS,
     )(returned, query, key, value, cotangent, gain)
     return (*outputs, skip_grad.reshape(channels), grad_rms[0, 0])

time: 73.6 us -> 74.3 us (level)
  no operation moved by 1% of the time
where the time goes in v6:
time: 74.3 us; the launch traced here: 72.9 us
  blocking collectives  56.8 us (76%)
  Pallas kernels  7.48 us (10%)
  starting transfers between devices  4.34 us (6%)
  waiting for transfers between devices  3.49 us (5%)
  between operations  0.75 us (1%)
    all_to_all x2, blocking collectives, exchange(): lax.all_to_all(array, 'seq', 0, 0, axis_index_groups=[ORDER], tiled=True)  56.8 us
    ppermute x3, starting transfers between devices, partner(): lax.ppermute(array, 'ch', [(i, i ^ bit) for i in range(lax.axis_size('ch'...  4.34 us
    ppermute x3, waiting for transfers between devices, partner(): lax.ppermute(array, 'ch', [(i, i ^ bit) for i in range(lax.axis_size('ch'...  3.49 us
    pallas_call x1, Pallas kernels, body(): pl.pallas_call(pre_kernel, out_shape=f32(BLOCKS, LINES, ROWS), in_specs=[...  2.17 us
    pallas_call x1, Pallas kernels, body(): pl.pallas_call(grad_kernel, out_shape=(f32(BLOCKS, CH_EACH, ROWS), f32(BL...  1.82 us
    pallas_call x1, Pallas kernels, body(): pl.pallas_call(functools.partial(post_kernel, count), out_shape=(*[bf16]...  1.76 us
  transfers between devices with their start and end apart: 3, of which 3 were waited for; matrix products, arithmetic and copies ran while one was open for 0% of the time, Pallas kernels for 2%

profile of v6, /device:TPU:32, one launch (start us, length us, event | category | flops | bytes accessed | tf_op | source)
XLA Modules:
  0.0 72.9 jit_solution(17218546170746360215)
XLA Ops:
  0.6 2.2 %shard_map.135 = f32[32,48,128]{2,1,0:T(8,128)} custom-call(bf16[128,512]{1,0:T(8,128)(2,1)} %q_ref.1, bf16[128,512]{1,0:T(8,128)(2,1)} %k_ref.1, bf16[128,512]{1,0:T(8,128)(2,1)} %v_ref.1, bf16[128,512]{1,0:T(8,128)(2,1)} %cot_ref.1, f32[128,512]{1,0:T(8,128)} %taps_hbm.1), custom_call_target="tpu_custom_call" | custom-call | tf_op jit(solution)/shard_map/pallas_call | solution.py:323
  2.8 0.0 copy-start.4
  2.8 0.0 copy-start.5
  2.8 0.0 copy-start.6
  2.8 30.1 %all_to_all.10.in_ref = f32[32,48,128]{2,1,0:T(8,128)S(1)} all-to-all(f32[32,48,128]{2,1,0:T(8,128)} %shard_map.135), channel_id=1, replica_groups={{184,160,216,232,80,176,96,8,0,192,224,152,48,144,168,88,16,248,128,208..., dimensions={0} | all-to-all | bytes 1572864 | tf_op jit(solution)/shard_map/all_to_all | solution.py:306
  33.0 0.0 copy-done.4
  33.0 0.0 copy-done.5
  33.0 0.0 copy-done.6
  33.0 1.8 %shard_map.136 = (f32[32,16,128]{2,1,0:T(8,128)S(1)}, f32[32,32,256]{2,1,0:T(8,128)S(1)}, f32[1,128]{1,0:T(1,128)S(1)}, f32[1,128]{1,0:T(1,128)S(1)}, f32[1,512]{1,0:T(1,128)S(1)}) custom-call(f32[32,48,128]{2,1,0:T(8,128)S(1)} %all_to_all.10.in_ref, f32[2,32,128]{2,1,0:T(8,128)S(1)} %copy-done.6, bf16[2,256,256]{2,1,0:T(8,128)(2,1)S(1)} %copy-done.5, ...), custom_call_target="tpu_custom_call" | custom-call | flops 2000000000 | bytes 4000000 | tf_op jit(solution)/shard_map/pallas_call | solution.py:338
  34.8 0.1 collective-permute-start
  34.9 0.6 shard_map.137.taps_ref
  35.5 0.5 collective-permute-done
  36.0 1.5 %collective-permute-start.1 = (f32[1,128]{1,0:T(1,128)S(1)}, f32[1,128]{1,0:T(1,128)S(1)}, u32[]{:S(2)}, u32[]{:S(2)}) collective-permute-start(f32[1,128]{1,0:T(1,128)S(1)} %add.6.after_ref), channel_id=1, source_target_pairs={{0,2},{1,3},{2,0},{3,1},{4,6},{5,7},{6,4},{7,5},{8,10},{9,11},{10,... | collective-permute-start | bytes 1544 | tf_op jit(solution)/shard_map/ppermute | solution.py:302
  37.5 0.5 shard_map.138.conv_ref
  38.0 1.5 %collective-permute-done.1 = f32[1,128]{1,0:T(1,128)S(1)} collective-permute-done((f32[1,128]{1,0:T(1,128)S(1)}, f32[1,128]{1,0:T(1,128)S(1)}, u32[]{:S(2)}, u32[]{:S(2)}) %collective-permute-start.1) | collective-permute-done | bytes 544 | tf_op jit(solution)/shard_map/ppermute | solution.py:302
  39.6 2.8 %collective-permute-start.2 = (f32[1,128]{1,0:T(1,128)S(1)}, f32[1,128]{1,0:T(1,128)S(1)}, u32[]{:S(2)}, u32[]{:S(2)}) collective-permute-start(f32[1,128]{1,0:T(1,128)S(1)} %add.7.after_ref.one_ref), channel_id=1, source_target_pairs={{0,6},{1,7},{2,4},{3,5},{4,2},{5,3},{6,0},{7,1},{8,14},{9,15},{10,... | collective-permute-start | bytes 1544 | tf_op jit(solution)/shard_map/ppermute | solution.py:302
  42.3 0.5 shard_map.139.back_ref
  42.9 1.5 %collective-permute-done.2.two_ref = f32[1,128]{1,0:T(1,128)S(1)} collective-permute-done((f32[1,128]{1,0:T(1,128)S(1)}, f32[1,128]{1,0:T(1,128)S(1)}, u32[]{:S(2)}, u32[]{:S(2)}) %collective-permute-start.2) | collective-permute-done | bytes 544 | tf_op jit(solution)/shard_map/ppermute | solution.py:302
  44.3 0.1 shard_map.140
  44.4 0.0 copy-start.1
  44.4 0.0 copy-start.2
  44.4 0.0 copy-start.3
  44.5 26.6 %all_to_all.11 = f32[32,49,1,128]{3,2,1,0:T(1,128)S(1)} all-to-all(f32[32,49,1,128]{3,2,1,0:T(1,128)S(1)} %bitcast.5), channel_id=1, replica_groups={{184,160,216,232,80,176,96,8,0,192,224,152,48,144,168,88,16,248,128,208..., dimensions={0} | all-to-all | bytes 1605632 | tf_op jit(solution)/shard_map/all_to_all | solution.py:306
  71.1 1.8 %shard_map.141 = (bf16[128,512]{1,0:T(8,128)(2,1)}, bf16[128,512]{1,0:T(8,128)(2,1)}, bf16[128,512]{1,0:T(8,128)(2,1)}, bf16[128,512]{1,0:T(8,128)(2,1)}, f32[12...) custom-call(f32[1568,128]{1,0:T(8,128)S(1)} %bitcast.6, bf16[128,512]{1,0:T(8,128)(2,1)S(1)} %copy-done, ...), custom_call_target="tpu_custom_call" | custom-call | tf_op jit(solution)/shard_map/pallas_call | solution.py:383
  (7 shorter events, 0.0 us)
Async XLA Ops:
  2.8 30.2 %copy-start.4 = (f32[512]{0:T(512)S(1)}, f32[512]{0:T(512)}, u32[]{:S(2)}) copy-start(f32[512]{0:T(512)} %param.13) | copy-start | bytes 6148
  2.8 30.2 %copy-start.5 = (bf16[2,256,256]{2,1,0:T(8,128)(2,1)S(1)}, bf16[2,256,256]{2,1,0:T(8,128)(2,1)}, u32[]{:S(2)}) copy-start(bf16[2,256,256]{2,1,0:T(8,128)(2,1)} %constant.5.clone.mat_ref) | copy-start | bytes 786436
  2.8 30.2 %copy-start.6 = (f32[2,32,128]{2,1,0:T(8,128)S(1)}, f32[2,32,128]{2,1,0:T(8,128)}, u32[]{:S(2)}) copy-start(f32[2,32,128]{2,1,0:T(8,128)} %constant.4.clone.tw_ref) | copy-start | bytes 98308
  34.8 1.2 %collective-permute-start = (f32[1,128]{1,0:T(1,128)S(1)}, f32[1,128]{1,0:T(1,128)S(1)}, u32[]{:S(2)}, u32[]{:S(2)}) collective-permute-start(f32[1,128]{1,0:T(1,128)S(1)} %get-tuple-element.20), channel_id=1, source_target_pairs={{0,1},{1,0},{2,3},{3,2},{4,5},{5,4},{6,7},{7,6},{8,9},{9,8},{10,11... | collective-permute-start | bytes 1544 | tf_op jit(solution)/shard_map/ppermute | solution.py:302
  36.0 3.5 %collective-permute-start.1 = (f32[1,128]{1,0:T(1,128)S(1)}, f32[1,128]{1,0:T(1,128)S(1)}, u32[]{:S(2)}, u32[]{:S(2)}) collective-permute-start(f32[1,128]{1,0:T(1,128)S(1)} %add.6.after_ref), channel_id=1, source_target_pairs={{0,2},{1,3},{2,0},{3,1},{4,6},{5,7},{6,4},{7,5},{8,10},{9,11},{10,... | collective-permute-start | bytes 1544 | tf_op jit(solution)/shard_map/ppermute | solution.py:302
  39.6 4.8 %collective-permute-start.2 = (f32[1,128]{1,0:T(1,128)S(1)}, f32[1,128]{1,0:T(1,128)S(1)}, u32[]{:S(2)}, u32[]{:S(2)}) collective-permute-start(f32[1,128]{1,0:T(1,128)S(1)} %add.7.after_ref.one_ref), channel_id=1, source_target_pairs={{0,6},{1,7},{2,4},{3,5},{4,2},{5,3},{6,0},{7,1},{8,14},{9,15},{10,... | collective-permute-start | bytes 1544 | tf_op jit(solution)/shard_map/ppermute | solution.py:302
  44.4 26.7 %copy-start = (bf16[128,512]{1,0:T(8,128)(2,1)S(1)}, bf16[128,512]{1,0:T(8,128)(2,1)}, u32[]{:S(2)}) copy-start(bf16[128,512]{1,0:T(8,128)(2,1)} %q_ref.1) | copy-start | bytes 393220
  44.4 26.7 %copy-start.1 = (bf16[128,512]{1,0:T(8,128)(2,1)S(1)}, bf16[128,512]{1,0:T(8,128)(2,1)}, u32[]{:S(2)}) copy-start(bf16[128,512]{1,0:T(8,128)(2,1)} %k_ref.1) | copy-start | bytes 393220
  44.4 26.7 %copy-start.2 = (bf16[128,512]{1,0:T(8,128)(2,1)S(1)}, bf16[128,512]{1,0:T(8,128)(2,1)}, u32[]{:S(2)}) copy-start(bf16[128,512]{1,0:T(8,128)(2,1)} %v_ref.1) | copy-start | bytes 393220
  44.4 26.7 %copy-start.3 = (bf16[128,512]{1,0:T(8,128)(2,1)S(1)}, bf16[128,512]{1,0:T(8,128)(2,1)}, u32[]{:S(2)}) copy-start(bf16[128,512]{1,0:T(8,128)(2,1)} %cot_ref.1) | copy-start | bytes 393220
